TPU v7x, 32 devices: a whole 2x2x4 slice. The times are simulated.
32 devices in a mesh: wide: 8 (over z, x), narrow: 4 (over y, core).
Axes of the slice: x: 2, y: 2, z: 4, core: 2. Of those that a mesh axis runs over, the one named last changes fastest.
Arguments:
- tokens: bfloat16 [16384, 2048], P(('wide', 'narrow')), may hold values from -6 to 6
- lengths: int32 [32], P(('wide', 'narrow')), may hold values from 1 to 512, 12288 in all
- in_weight: bfloat16 [2048, 8512], P(('wide', 'narrow')), may hold values from -0.125 to 0.125
- out_weight: bfloat16 [4096, 2048], P(('wide', 'narrow')), may hold values from -0.09375 to 0.09375
- norm_gain: bfloat16 [2048], P(('wide', 'narrow')), may hold values from 0.5 to 1.5
- conv_weight: bfloat16 [4352, 4], P(('wide', 'narrow')), may hold values from -3 to 3
- conv_bias: bfloat16 [4352], P(('wide', 'narrow')), may hold values from -0.5 to 0.5
- out_gain: bfloat16 [4096], P(('wide', 'narrow')), may hold values from 0.5 to 1.5
- a_log: float32 [64], P('wide'), may hold values from -3 to 1.6
- dt_bias: float32 [64], P('wide'), may hold values from -6 to -3
- d_skip: float32 [64], P('wide'), may hold values from 0.5 to 1.5
- cotangent: bfloat16 [16384, 2048], P(('wide', 'narrow')), may hold values from -6 to 6
Outputs:
- output: bfloat16 [16384, 2048], P(('wide', 'narrow'))
- token_grad: bfloat16 [16384, 2048], P(('wide', 'narrow'))
- in_weight_grad: float32 [2048, 8512], P(('wide', 'narrow'))
- out_weight_grad: float32 [4096, 2048], P(('wide', 'narrow'))
- norm_gain_grad: float32 [2048], P(('wide', 'narrow'))
- conv_weight_grad: float32 [4352, 4], P(('wide', 'narrow'))
- conv_bias_grad: float32 [4352], P(('wide', 'narrow'))
- out_gain_grad: float32 [4096], P(('wide', 'narrow'))
- a_log_grad: float32 [64], P('wide')
- dt_bias_grad: float32 [64], P('wide')
- d_skip_grad: float32 [64], P('wide')
Inputs may be any that keep to these rules, and one draw needn't show every extreme that they name: `lengths`: each sequence's live tokens are the first rows of its 512 slots; the longest fills all of them.
All inputs are finite; a program needn't handle non-finite values. No bound on the sum of `lengths` on one device may be relied on, other than what follows from the above.
Results may differ from a plain program's by a relative error of at most 0.014.
Values may be sent and summed in bfloat16 or wider, within the bound.
No kernel may reach another device: no remote copies, remote signals or barrier semaphores. Data moves between devices by JAX's collectives and lax.ppermute only.
A program may use at most 448 MiB of HBM per device.

v0:
```python
from functools import partial

import jax
import jax.numpy as jnp
from jax import lax
from jax.sharding import PartitionSpec as P

HEADS = 64
HEAD_DIM = 64
NSTATE = 128
KCONV = 4
SPAN = 256


EPS = 1e-05


def rounded(values):
    fixed = lax.stop_gradient(values)
    coarse = lax.optimization_barrier(fixed.astype(jnp.bfloat16)).astype(jnp.float32)
    return values + (coarse - fixed)


def rms_scale(values, gain_vec):
    return values * lax.rsqrt(jnp.mean(values * values, axis=-1, keepdims=True) + EPS) * gain_vec


def block_step(carry_state, pieces, rounding):
    x_rows, b_rows, c_rows, dt_rows, log_decay = pieces
    block_len = x_rows.shape[0]
    head_count = dt_rows.shape[1]
    cum_decay = jnp.cumsum(log_decay, axis=0).T
    c_dot_b = jnp.dot(c_rows, b_rows.T, preferred_element_type=jnp.float32)
    lower_mask = (
        lax.iota(jnp.int32, block_len)[:, None] >= lax.iota(jnp.int32, block_len)[None, :]
    )[None]
    spread_log = cum_decay[:, :, None] - cum_decay[:, None, :]
    decays = jnp.where(lower_mask, jnp.exp(jnp.where(lower_mask, spread_log, 0.0)), 0.0)
    mixing = rounding(c_dot_b[None] * decays * dt_rows.T[:, None, :])
    x_heads = x_rows.reshape(block_len, head_count, -1)
    within = jnp.einsum("hts,shp->thp", mixing, x_heads, preferred_element_type=jnp.float32)
    carried = (
        jnp.einsum("tn,hnp->thp", c_rows, carry_state, preferred_element_type=jnp.float32)
        * jnp.exp(cum_decay).T[:, :, None]
    )
    end_decay = cum_decay[:, -1:]
    entry_scale = jnp.exp(end_decay - cum_decay) * dt_rows.T
    fresh_state = jnp.einsum(
        "sn,hs,shp->hnp", b_rows, entry_scale, x_heads, preferred_element_type=jnp.float32
    )
    carry_state = carry_state * jnp.exp(end_decay)[:, :, None] + fresh_state
    return (carry_state, (within + carried).reshape(block_len, -1))


def ssd_mixer(projected, conv_w, conv_b, log_rate, rate_bias, skip_gain, gain_out, rounding):
    seq_len = projected.shape[0]
    inner_width = HEADS * HEAD_DIM
    channels = inner_width + 2 * NSTATE
    gate_part = projected[:, :inner_width]
    conv_in = projected[:, inner_width : inner_width + channels]
    dt_raw = projected[:, inner_width + channels :]
    padded = jnp.pad(conv_in, ((KCONV - 1, 0), (0, 0)))
    conv_out = conv_b
    for tap_idx in range(KCONV):
        conv_out = conv_out + padded[tap_idx : tap_idx + seq_len] * conv_w[:, tap_idx]
    active = jax.nn.silu(conv_out)
    x_rows = rounding(active[:, :inner_width])
    b_rows = rounding(active[:, inner_width : inner_width + NSTATE])
    c_rows = rounding(active[:, inner_width + NSTATE :])
    dt_rows = jax.nn.softplus(dt_raw + rate_bias)
    log_decay = -dt_rows * jnp.exp(log_rate)
    block_count = seq_len // SPAN

    def to_blocks(values):
        return values.reshape(block_count, SPAN, values.shape[1])

    zero_state = jnp.zeros((HEADS, NSTATE, HEAD_DIM), jnp.float32)
    _, block_outs = lax.scan(
        jax.checkpoint(partial(block_step, rounding=rounding)),
        zero_state,
        (
            to_blocks(x_rows),
            to_blocks(b_rows),
            to_blocks(c_rows),
            to_blocks(dt_rows),
            to_blocks(log_decay),
        ),
    )
    ssd_out = block_outs.reshape(seq_len, inner_width) + x_rows * jnp.repeat(skip_gain, HEAD_DIM)
    gated_out = ssd_out * jax.nn.silu(gate_part)
    return rms_scale(gated_out, gain_out)


def fetch_weights(in_part, out_part, norm_part, conv_part, bias_part, gain_part):
    return (
        lax.all_gather(in_part, ("wide", "narrow"), axis=0, tiled=True),
        lax.all_gather(out_part, ("wide", "narrow"), axis=0, tiled=True),
        lax.all_gather(norm_part, ("wide", "narrow"), axis=0, tiled=True),
        lax.all_gather(conv_part, ("wide", "narrow"), axis=0, tiled=True),
        lax.all_gather(bias_part, ("wide", "narrow"), axis=0, tiled=True),
        lax.all_gather(gain_part, ("wide", "narrow"), axis=0, tiled=True),
    )


def spread_heads(head_grad, wide_count, narrow_count):
    share_len = head_grad.shape[0] // wide_count
    blocks = jnp.broadcast_to(
        head_grad.reshape(wide_count, 1, share_len), (wide_count, narrow_count, share_len)
    )
    return blocks.reshape(-1)


def settle_grads(
    normed_low,
    proj_grad,
    mixed_low,
    branch_grad,
    norm_term,
    conv_term,
    bias_term,
    gain_term,
    head_terms,
):
    wide_count = lax.axis_size("wide")
    narrow_count = lax.axis_size("narrow")
    heads_laid = [spread_heads(head_term, wide_count, narrow_count) for head_term in head_terms]
    columns = normed_low
    inw_own = lax.psum_scatter(
        lax.dot_general(
            columns, proj_grad, (((0,), (0,)), ((), ())), preferred_element_type=jnp.float32
        ),
        ("wide", "narrow"),
        scatter_dimension=0,
        tiled=True,
    )
    columns = mixed_low
    outw_own = lax.psum_scatter(
        lax.dot_general(
            columns, branch_grad, (((0,), (0,)), ((), ())), preferred_element_type=jnp.float32
        ),
        ("wide", "narrow"),
        scatter_dimension=0,
        tiled=True,
    )
    small_own = (
        lax.psum_scatter(norm_term, ("wide", "narrow"), scatter_dimension=0, tiled=True),
        lax.psum_scatter(conv_term, ("wide", "narrow"), scatter_dimension=0, tiled=True),
        lax.psum_scatter(bias_term, ("wide", "narrow"), scatter_dimension=0, tiled=True),
        lax.psum_scatter(gain_term, ("wide", "narrow"), scatter_dimension=0, tiled=True),
        lax.psum_scatter(heads_laid[0], ("wide", "narrow"), scatter_dimension=0, tiled=True),
        lax.psum_scatter(heads_laid[1], ("wide", "narrow"), scatter_dimension=0, tiled=True),
        lax.psum_scatter(heads_laid[2], ("wide", "narrow"), scatter_dimension=0, tiled=True),
    )
    return (inw_own, outw_own) + tuple(small_own)


def body(
    tokens,
    lengths,
    in_weight,
    out_weight,
    norm_gain,
    conv_weight,
    conv_bias,
    out_gain,
    a_log,
    dt_bias,
    d_skip,
    cotangent,
):
    row_count = tokens.shape[0]
    live_mask = (lax.iota(jnp.int32, row_count) < lengths[0]).astype(jnp.float32)[:, None]
    gathered = fetch_weights(in_weight, out_weight, norm_gain, conv_weight, conv_bias, out_gain)
    head_values = (
        lax.all_gather(a_log, "wide", axis=0, tiled=True),
        lax.all_gather(dt_bias, "wide", axis=0, tiled=True),
        lax.all_gather(d_skip, "wide", axis=0, tiled=True),
    )
    source = tokens.astype(jnp.float32)
    normed, front_back = jax.vjp(rms_scale, source, gathered[2].astype(jnp.float32))
    normed_low = normed.astype(jnp.bfloat16)
    projected = jnp.dot(normed_low, gathered[0], preferred_element_type=jnp.float32)

    def mix_local(proj_rows, conv_w, conv_b, log_rate, rate_bias, skip_gain, gain_out):
        return ssd_mixer(
            proj_rows, conv_w, conv_b, log_rate, rate_bias, skip_gain, gain_out, rounded
        )

    mixed, mix_back = jax.vjp(
        mix_local,
        projected,
        gathered[3].astype(jnp.float32),
        gathered[4].astype(jnp.float32),
        head_values[0],
        head_values[1],
        head_values[2],
        gathered[5].astype(jnp.float32),
    )
    mixed_low = mixed.astype(jnp.bfloat16)
    branch = jnp.dot(mixed_low, gathered[1], preferred_element_type=jnp.float32)
    output = (source + live_mask * branch).astype(jnp.bfloat16)
    gathered = fetch_weights(in_weight, out_weight, norm_gain, conv_weight, conv_bias, out_gain)
    cot_rows = cotangent.astype(jnp.float32)
    branch_grad = (live_mask * cot_rows).astype(jnp.bfloat16)
    mixed_grad = lax.dot_general(
        branch_grad, gathered[1], (((1,), (1,)), ((), ())), preferred_element_type=jnp.float32
    )
    mix_grads = mix_back(mixed_grad)
    proj_grad = mix_grads[0].astype(jnp.bfloat16)
    normed_grad = lax.dot_general(
        proj_grad, gathered[0], (((1,), (1,)), ((), ())), preferred_element_type=jnp.float32
    )
    source_grad, normgain_grad = front_back(normed_grad)
    token_grad = (cot_rows + source_grad).astype(jnp.bfloat16)
    owned = settle_grads(
        normed_low,
        proj_grad,
        mixed_low,
        branch_grad,
        normgain_grad,
        mix_grads[1],
        mix_grads[2],
        mix_grads[6],
        (mix_grads[3], mix_grads[4], mix_grads[5]),
    )
    return (
        output,
        token_grad,
        owned[0],
        owned[1],
        owned[2],
        owned[3],
        owned[4],
        owned[5],
        owned[6],
        owned[7],
        owned[8],
    )


def solution(mesh):
    in_specs = (
        P(("wide", "narrow"), None),
        P(("wide", "narrow")),
        P(("wide", "narrow"), None),
        P(("wide", "narrow"), None),
        P(("wide", "narrow")),
        P(("wide", "narrow"), None),
        P(("wide", "narrow")),
        P(("wide", "narrow")),
        P("wide"),
        P("wide"),
        P("wide"),
        P(("wide", "narrow"), None),
    )
    out_specs = (
        P(("wide", "narrow"), None),
        P(("wide", "narrow"), None),
        P(("wide", "narrow"), None),
        P(("wide", "narrow"), None),
        P(("wide", "narrow")),
        P(("wide", "narrow"), None),
        P(("wide", "narrow")),
        P(("wide", "narrow")),
        P("wide"),
        P("wide"),
        P("wide"),
    )
    return jax.shard_map(body, mesh=mesh, in_specs=in_specs, out_specs=out_specs, check_vma=False)
```

profile of v0, /device:TPU:1, one launch (start us, length us, event | category | flops | bytes accessed | tf_op | source)
XLA Modules:
  0.0 2244.8 jit_solution(11911795497992488165)
XLA Ops:
  13.8 19.4 all-reduce.29
  35.5 45.5 %all-reduce.30 = (bf16[2048]{0:T(1024)(128)(2,1)S(1)}, bf16[4352]{0:T(1024)(128)(2,1)S(1)}) all-reduce(bf16[2048]{0:T(1024)(128)(2,1)S(1)} %dynamic-update-slice, bf16[4352]{0:T(1024)(128)(2,1)S(1)} %dynamic-update-slice.3), channel_id=1, replica_groups=mesh['wide'=8,'narrow'=4] {'wide','narrow'}, use_global_device_ids=true, to_apply=%add.16 | all-reduce | flops 6400 | bytes 25600
  81.0 42.1 %all-gather.1 = bf16[32,1,128]{2,1,0:T(2,128)(2,1)S(1)} all-gather(bf16[1,1,128]{2,1,0:T(2,128)(2,1)} %bitcast.427), channel_id=1, replica_groups=mesh['wide'=8,'narrow'=4] {'wide','narrow'}, dimensions={0}, use_global_device_ids=true | all-gather | bytes 8448 | tf_op jit(solution)/shard_map/all_gather | solution.py:101
  124.4 39.0 %all-gather = bf16[32,136,4]{1,2,0:T(4,128)(2,1)S(1)} all-gather(bf16[1,136,4]{1,2,0:T(4,128)(2,1)} %bitcast.426), channel_id=1, replica_groups=mesh['wide'=8,'narrow'=4] {'wide','narrow'}, dimensions={0}, use_global_device_ids=true | all-gather | bytes 35904 | tf_op jit(solution)/shard_map/all_gather | solution.py:99
  166.5 50.2 %all-gather.5.cloned.1.call-done = bf16[2048,8512]{1,0:T(8,128)(2,1)} async-done(((bf16[64,8512]{1,0:T(8,128)(2,1)}), bf16[2048,8512]{1,0:T(8,128)(2,1)}) %all-gather.5.cloned.1.call-update) | async-done | bytes 34865168 | tf_op jit(solution)/shard_map/all_gather | solution.py:96
  216.6 26.3 %fusion.102 = f32[512,8512]{0,1:T(8,128)} fusion(bf16[2048,8512]{1,0:T(8,128)(2,1)} %all-gather.5.cloned.1.call-done, bf16[512,2048]{1,0:T(8,128)(2,1)} %param.16, f32[2048]{0:T(1024)S(1)} %convert_element_type.95, f32[512]{0:T(512)S(1)} %fusion.108), kind=kOutput, calls=%fused_computation.183 | convolution fusion | flops 17855152128 | bytes 54405120 | tf_op jit(solution)/shard_map/dot_general | solution.py:182
  242.9 8.0 slice.132
  253.4 23.5 %fusion.81 = (f32[512,4352]{0,1:T(8,128)S(1)}, f32[512,4352]{0,1:T(8,128)}) fusion(f32[512,4352]{0,1:T(8,128)} %slice.132, f32[4352]{0:T(1024)S(1)} %get-tuple-element.725, f32[4352]{0:T(1024)S(1)} %get-tuple-element.726, f32[4352]{0:T(1024)S(1)} %get-tuple-element.727, f32[4352]{0:T(1024)S(1)} %get-tuple-element.724, f32[4352]{0:T(1024)S(1)} %convert_element_type.97), kind=kLoop, calls=%fused_computation.142 | loop fusion | flops 26738688 | bytes 26825728 | tf_op jit(solution)/shard_map/jvp(jit(silu))/mul | solution.py:66
  285.0 6.1 subtract_add_fusion.8
  297.0 5.4 broadcast.177.clone2
  302.4 257.3 %while.44 = (s32[]{:T(128)}, f32[64,128,64]{1,2,0:T(8,128)S(1)}, f32[2,256,4096]{1,0,2:T(2,128)}, f32[2,64,128,64]{2,3,1,0:T(8,128)}, f32[2,256,64]{1,2,0:T(8,12...) while((s32[]{:T(128)}, f32[64,128,64]{1,2,0:T(8,128)S(1)}, ...), condition=%wide.region_4.5_spmd.clone.clone, body=%wide.region_1.4_spmd.clone.clone.sunk | while | flops 1156104448 | bytes 122035080 | solution.py:78
  315.3 5.1 fusion.220
  320.4 8.3 bitcast_add_fusion.14
  328.7 19.2 copy.361
  347.9 83.3 %dynamic_update_slice.87 = f32[2,256,4096]{1,0,2:T(2,128)} dynamic-update-slice(f32[2,256,4096]{1,0,2:T(2,128)} %get-tuple-element.1047, f32[1,256,4096]{1,0,2:T(1,128)} %copy.361, s32[]{:T(128)S(6)} %copy.378, s32[]{:T(128)} %constant.121.clone.1..sunk.1, s32[]{:T(128)} %constant.121.clone.1..sunk.1) | dynamic-update-slice | bytes 8388612 | tf_op jit(solution)/shard_map/jvp()/while/body/jit(dynamic_update_index_in_dim)/dynamic_update_slice | solution.py:78
  443.8 5.1 fusion.220
  448.9 8.1 bitcast_add_fusion.14
  457.0 19.2 copy.361
  476.2 83.3 %dynamic_update_slice.87 = f32[2,256,4096]{1,0,2:T(2,128)} dynamic-update-slice(f32[2,256,4096]{1,0,2:T(2,128)} %get-tuple-element.1047, f32[1,256,4096]{1,0,2:T(1,128)} %copy.361, s32[]{:T(128)S(6)} %copy.378, s32[]{:T(128)} %constant.121.clone.1..sunk.1, s32[]{:T(128)} %constant.121.clone.1..sunk.1) | dynamic-update-slice | bytes 8388612 | tf_op jit(solution)/shard_map/jvp()/while/body/jit(dynamic_update_index_in_dim)/dynamic_update_slice | solution.py:78
  559.7 4.6 copy.296
  565.8 9.0 multiply_reduce_fusion.12
  575.0 17.8 multiply_reduce_fusion.10
  592.8 18.2 multiply_reduce_fusion.9
  611.0 10.6 reshape.410
  624.5 5.4 broadcast.177.clone
  629.9 342.9 %while.43 = (s32[]{:T(128)}, f32[64,128,64]{1,2,0:T(8,128)}, f32[2,256,4096]{1,0,2:T(2,128)}, f32[2,256,128]{2,1,0:T(8,128)}, f32[2,256,128]{2,1,0:T(8,128)}, /*...) while((s32[]{:T(128)}, f32[64,128,64]{1,2,0:T(8,128)}, ...), condition=%wide.region_19.20_spmd.clone, body=%wide.region_7.19_spmd.clone.sunk | while | flops 2587640576 | bytes 238366704 | solution.py:78
  651.9 5.0 multiply_reduce_fusion.18
  657.1 16.5 fusion.204
  677.7 11.3 bitcast_add_fusion.12
  693.4 19.1 copy.353
  717.0 83.3 %dynamic_update_slice.84 = f32[2,256,4096]{1,0,2:T(2,128)} dynamic-update-slice(f32[2,256,4096]{1,0,2:T(2,128)} %get-tuple-element.1090, f32[1,256,4096]{1,0,2:T(1,128)} %copy.353, s32[]{:T(128)S(6)} %sub.332, s32[]{:T(128)} %constant.121.clone.1..sunk, s32[]{:T(128)} %constant.121.clone.1..sunk) | dynamic-update-slice | bytes 8388612 | tf_op jit(solution)/shard_map/transpose(jvp())/while/body/jit(dynamic_update_index_in_dim)/dynamic_update_slice | solution.py:78
  824.2 5.0 multiply_reduce_fusion.18
  829.4 16.5 fusion.204
  850.0 11.3 bitcast_add_fusion.12
  865.7 19.1 copy.353
  889.3 83.3 %dynamic_update_slice.84 = f32[2,256,4096]{1,0,2:T(2,128)} dynamic-update-slice(f32[2,256,4096]{1,0,2:T(2,128)} %get-tuple-element.1090, f32[1,256,4096]{1,0,2:T(1,128)} %copy.353, s32[]{:T(128)S(6)} %sub.332, s32[]{:T(128)} %constant.121.clone.1..sunk, s32[]{:T(128)} %constant.121.clone.1..sunk) | dynamic-update-slice | bytes 8388612 | tf_op jit(solution)/shard_map/transpose(jvp())/while/body/jit(dynamic_update_index_in_dim)/dynamic_update_slice | solution.py:78
  979.3 6.0 multiply_add_fusion.1
  985.3 28.9 %multiply_reduce_fusion.7 = (f32[4352]{0:T(1024)S(1)}, f32[4352]{0:T(1024)S(1)}, f32[4352]{0:T(1024)S(1)}, f32[4352]{0:T(1024)}, f32[4352]{0:T(1024)S(1)}, /*index=5*/f32[512,4352]{0,1:T(8,128)}) fusion(f32[512,4352]{0,1:T(8,128)} %slice.132, f32[512,8512]{0,1:T(8,128)} %fusion.102, f32[512,4352]{0,1:T(8,128)} %get-tuple-element.797, ...), kind=kLoop, calls=%fused_computation.139 | loop fusion | flops 44542720 | bytes 44651520 | tf_op jit(solution)/shard_map/transpose(jvp())/reduce_sum | solution.py:65
  1015.1 19.0 fusion.96
  1036.4 12.4 broadcast_multiply_fusion
  1048.8 14.6 pad_add_fusion
  1063.4 33.8 %fusion.100 = f32[2048,8512]{1,0:T(8,128)} fusion(bf16[512,2048]{1,0:T(8,128)(2,1)S(1)} %copy-done.13, f32[2048]{0:T(1024)S(1)} %copy-done.51, f32[512]{0:T(512)S(1)} %copy-done.58, f32[512,4096]{0,1:T(8,128)} %get-tuple-element.814, f32[512,4352]{0,1:T(8,128)} %pad_add_fusion, f32[512,64]{0,1:T(8,128)S(1)} %get-tuple-element.792), kind=kOutput, calls=%fused_computation.182 | convolution fusion | flops 17868226560 | bytes 89270272 | tf_op jit(solution)/shard_map/dot_general | solution.py:129
  1098.7 36.1 %fusion.88 = (f32[2048]{0:T(1024)S(1)}, f32[512]{0:T(512)S(1)}, f32[512,2048]{1,0:T(8,128)}) fusion(bf16[512,2048]{1,0:T(8,128)(2,1)S(1)} %copy-done.13, f32[512]{0:T(512)S(1)} %copy-done.58, f32[2048]{0:T(1024)S(1)} %copy-done.51, bf16[2048,8512]{1,0:T(8,128)(2,1)} %all-gather.5.cloned.1.call-done, f32[512,4096]{0,1:T(8,128)} %get-tuple-element.814, ...), kind=kOutput, calls=%fused_computation.172 | convolution fusion | flops 17871370240 | bytes 58609664 | tf_op jit(solution)/shard_map/dot_general | solution.py:210
  1134.8 51.2 %all-reduce.28 = (f32[2048]{0:T(1024)S(1)}, f32[4352]{0:T(1024)S(1)}, f32[4096]{0:T(1024)S(1)}, f32[256]{0:T(256)S(1)}, f32[256]{0:T(256)S(1)}, /*index=5*/f32[256]{0:T(256)S(1)}) all-reduce(f32[2048]{0:T(1024)S(1)} %get-tuple-element.722, f32[4352]{0:T(1024)S(1)} %copy-done.46, ...), channel_id=4, replica_groups=mesh['wide'=8,'narrow'=4] {'wide','narrow'}, use_global_device_ids=true, to_apply=%region_24.25.clone | all-reduce | flops 11264 | bytes 90112
  1189.5 5.6 fusion.90
  1195.1 16.2 fusion.92
  1212.7 283.7 %reduce-scatter.6.cloned.1.call-done = f32[128,2048]{1,0:T(8,128)} async-done(((f32[4096,2048]{1,0:T(8,128)}), f32[128,2048]{1,0:T(8,128)}) %reduce-scatter.6.cloned.1.call-update) | async-done | bytes 1048592 | tf_op jit(solution)/shard_map/reduce_scatter | solution.py:137
  1496.4 741.4 %reduce-scatter.4.cloned.1.call-done = f32[64,8512]{1,0:T(8,128)} async-done(((f32[2048,8512]{1,0:T(8,128)}), f32[64,8512]{1,0:T(8,128)}) %reduce-scatter.4.cloned.1.call-update) | async-done | bytes 2179088 | tf_op jit(solution)/shard_map/reduce_scatter | solution.py:128
  (397 shorter events, 144.5 us)
Async XLA Ops:
  7.2 209.5 %all-gather.5.cloned.1.call-start = ((), (), s32[]{:S(2)}) async-start(), calls=%async_computation.2 | async-start | bytes 36225024 | tf_op jit(solution)/shard_map/all_gather | solution.py:96
  7.9 567.0 %all-gather.7.cloned.1.call-start = ((), (), s32[]{:S(2)}) async-start(), calls=%async_computation.3 | async-start | bytes 17301504 | tf_op jit(solution)/shard_map/all_gather | solution.py:97
  8.7 1202.6 %all-reduce.33.cloned.1.call-start = ((), (), s32[]{:S(2)}) async-start(), calls=%async_computation.6 | async-start | bytes 139264
  33.3 217.7 %copy-start.59 = (f32[64]{0:T(128)}, f32[64]{0:T(128)S(1)}, u32[]{:S(2)}) copy-start(f32[64]{0:T(128)S(1)} %get-tuple-element.782) | copy-start | bytes 772
  33.3 217.6 %copy-start.61 = (f32[64]{0:T(128)}, f32[64]{0:T(128)S(1)}, u32[]{:S(2)}) copy-start(f32[64]{0:T(128)S(1)} %exp.80) | copy-start | bytes 772
  81.0 162.0 %copy-start.50 = (f32[2048]{0:T(1024)}, f32[2048]{0:T(1024)S(1)}, u32[]{:S(2)}) copy-start(f32[2048]{0:T(1024)S(1)} %convert_element_type.95) | copy-start | bytes 24580
  164.3 89.1 %copy-start.38 = (f32[4352]{0:T(1024)}, f32[4352]{0:T(1024)S(1)}, u32[]{:S(2)}) copy-start(f32[4352]{0:T(1024)S(1)} %get-tuple-element.724) | copy-start | bytes 52228
  164.3 89.1 %copy-start.40 = (f32[4352]{0:T(1024)}, f32[4352]{0:T(1024)S(1)}, u32[]{:S(2)}) copy-start(f32[4352]{0:T(1024)S(1)} %get-tuple-element.725) | copy-start | bytes 52228
  164.3 89.1 %copy-start.42 = (f32[4352]{0:T(1024)}, f32[4352]{0:T(1024)S(1)}, u32[]{:S(2)}) copy-start(f32[4352]{0:T(1024)S(1)} %get-tuple-element.726) | copy-start | bytes 52228
  164.3 89.1 %copy-start.44 = (f32[4352]{0:T(1024)}, f32[4352]{0:T(1024)S(1)}, u32[]{:S(2)}) copy-start(f32[4352]{0:T(1024)S(1)} %get-tuple-element.727) | copy-start | bytes 52228
  166.4 76.5 %copy-start.52 = (f32[512]{0:T(512)}, f32[512]{0:T(512)S(1)}, u32[]{:S(2)}) copy-start(f32[512]{0:T(512)S(1)} %fusion.91) | copy-start | bytes 6148
  166.5 76.5 %copy-start.57 = (f32[512]{0:T(512)}, f32[512]{0:T(512)S(1)}, u32[]{:S(2)}) copy-start(f32[512]{0:T(512)S(1)} %fusion.108) | copy-start | bytes 6148
  252.0 24.9 %copy-start.24 = (f32[512,64]{0,1:T(8,128)}, f32[512,64]{0,1:T(8,128)S(1)}, u32[]{:S(2)}) copy-start(f32[512,64]{0,1:T(8,128)S(1)} %get-tuple-element.799) | copy-start | bytes 393220
  347.9 83.3 %copy-start.8 = (f32[64,128,64]{1,2,0:T(8,128)S(1)}, f32[64,128,64]{1,2,0:T(8,128)}, u32[]{:S(2)}) copy-start(f32[64,128,64]{1,2,0:T(8,128)} %bitcast_add_fusion.13) | copy-start | bytes 6291460 | tf_op jit(solution)/shard_map/jvp()/while
  347.9 83.3 %copy-start.18 = (pred[256,256]{1,0:T(8,128)(4,1)S(1)}, pred[256,256]{1,0:T(8,128)(4,1)}, u32[]{:S(2)}) copy-start(pred[256,256]{1,0:T(8,128)(4,1)} %copy-done.17) | copy-start | bytes 196612 | tf_op jit(solution)/shard_map/jvp()/while
  476.2 83.3 %copy-start.8 = (f32[64,128,64]{1,2,0:T(8,128)S(1)}, f32[64,128,64]{1,2,0:T(8,128)}, u32[]{:S(2)}) copy-start(f32[64,128,64]{1,2,0:T(8,128)} %bitcast_add_fusion.13) | copy-start | bytes 6291460 | tf_op jit(solution)/shard_map/jvp()/while
  476.2 83.3 %copy-start.18 = (pred[256,256]{1,0:T(8,128)(4,1)S(1)}, pred[256,256]{1,0:T(8,128)(4,1)}, u32[]{:S(2)}) copy-start(pred[256,256]{1,0:T(8,128)(4,1)} %copy-done.17) | copy-start | bytes 196612 | tf_op jit(solution)/shard_map/jvp()/while
  630.3 26.8 %copy-start.23 = (pred[256,256]{1,0:T(8,128)(4,1)}, pred[256,256]{1,0:T(8,128)(4,1)S(1)}, u32[]{:S(2)}) copy-start(pred[256,256]{1,0:T(8,128)(4,1)S(1)} %iota_compare_fusion.4) | copy-start | bytes 196612 | tf_op jit(solution)/shard_map/transpose(jvp())/while
  651.9 21.8 copy-start.16
  691.2 21.3 copy-start.28
  691.2 21.5 copy-start.26
  691.3 25.6 %copy-start.21 = (f32[64,256]{1,0:T(8,128)S(1)}, f32[64,256]{1,0:T(8,128)}, u32[]{:S(2)}) copy-start(f32[64,256]{1,0:T(8,128)} %get-tuple-element.1014) | copy-start | bytes 196612 | tf_op jit(solution)/shard_map/transpose(jvp())/while
  693.4 22.5 %copy-start.33 = (f32[2,256,64]{1,0,2:T(2,128)S(1)}, f32[2,256,64]{1,0,2:T(2,128)}, u32[]{:S(2)}) copy-start(f32[2,256,64]{1,0,2:T(2,128)} %get-tuple-element.1094) | copy-start | bytes 393220 | tf_op jit(solution)/shard_map/transpose(jvp())/while
  693.4 23.6 %copy-start.30 = (f32[2,256,64]{2,1,0:T(8,128)S(1)}, f32[2,256,64]{2,1,0:T(8,128)}, u32[]{:S(2)}) copy-start(f32[2,256,64]{2,1,0:T(8,128)} %get-tuple-element.1093) | copy-start | bytes 393220 | tf_op jit(solution)/shard_map/transpose(jvp())/while
  712.7 87.5 %copy-start.29 = (f32[2,256,128]{2,1,0:T(8,128)}, f32[2,256,128]{2,1,0:T(8,128)S(1)}, u32[]{:S(2)}) copy-start(f32[2,256,128]{2,1,0:T(8,128)S(1)} %fusion.208) | copy-start | bytes 786436 | tf_op jit(solution)/shard_map/transpose(jvp())/while
  712.9 87.3 %copy-start.27 = (f32[2,256,128]{2,1,0:T(8,128)}, f32[2,256,128]{2,1,0:T(8,128)S(1)}, u32[]{:S(2)}) copy-start(f32[2,256,128]{2,1,0:T(8,128)S(1)} %fusion.210) | copy-start | bytes 786436 | tf_op jit(solution)/shard_map/transpose(jvp())/while
  716.8 83.4 %copy-start.34 = (f32[2,256,64]{1,0,2:T(2,128)}, f32[2,256,64]{1,0,2:T(2,128)S(1)}, u32[]{:S(2)}) copy-start(f32[2,256,64]{1,0,2:T(2,128)S(1)} %dynamic_update_slice.85) | copy-start | bytes 393220 | tf_op jit(solution)/shard_map/transpose(jvp())/while
  717.0 83.3 %copy-start.31 = (f32[2,256,64]{2,1,0:T(8,128)}, f32[2,256,64]{2,1,0:T(8,128)S(1)}, u32[]{:S(2)}) copy-start(f32[2,256,64]{2,1,0:T(8,128)S(1)} %bitcast_dynamic-update-slice_fusion.4) | copy-start | bytes 393220 | tf_op jit(solution)/shard_map/transpose(jvp())/while
  800.3 29.1 %copy-start.23 = (pred[256,256]{1,0:T(8,128)(4,1)}, pred[256,256]{1,0:T(8,128)(4,1)S(1)}, u32[]{:S(2)}) copy-start(pred[256,256]{1,0:T(8,128)(4,1)S(1)} %iota_compare_fusion.4) | copy-start | bytes 196612 | tf_op jit(solution)/shard_map/transpose(jvp())/while
  824.2 21.8 copy-start.16
  863.6 21.3 copy-start.28
  863.6 21.5 copy-start.26
  863.6 25.6 %copy-start.21 = (f32[64,256]{1,0:T(8,128)S(1)}, f32[64,256]{1,0:T(8,128)}, u32[]{:S(2)}) copy-start(f32[64,256]{1,0:T(8,128)} %get-tuple-element.1014) | copy-start | bytes 196612 | tf_op jit(solution)/shard_map/transpose(jvp())/while
  865.7 22.5 %copy-start.33 = (f32[2,256,64]{1,0,2:T(2,128)S(1)}, f32[2,256,64]{1,0,2:T(2,128)}, u32[]{:S(2)}) copy-start(f32[2,256,64]{1,0,2:T(2,128)} %get-tuple-element.1094) | copy-start | bytes 393220 | tf_op jit(solution)/shard_map/transpose(jvp())/while
  865.7 23.6 %copy-start.30 = (f32[2,256,64]{2,1,0:T(8,128)S(1)}, f32[2,256,64]{2,1,0:T(8,128)}, u32[]{:S(2)}) copy-start(f32[2,256,64]{2,1,0:T(8,128)} %get-tuple-element.1093) | copy-start | bytes 393220 | tf_op jit(solution)/shard_map/transpose(jvp())/while
  885.1 87.5 %copy-start.29 = (f32[2,256,128]{2,1,0:T(8,128)}, f32[2,256,128]{2,1,0:T(8,128)S(1)}, u32[]{:S(2)}) copy-start(f32[2,256,128]{2,1,0:T(8,128)S(1)} %fusion.208) | copy-start | bytes 786436 | tf_op jit(solution)/shard_map/transpose(jvp())/while
  885.2 87.3 %copy-start.27 = (f32[2,256,128]{2,1,0:T(8,128)}, f32[2,256,128]{2,1,0:T(8,128)S(1)}, u32[]{:S(2)}) copy-start(f32[2,256,128]{2,1,0:T(8,128)S(1)} %fusion.210) | copy-start | bytes 786436 | tf_op jit(solution)/shard_map/transpose(jvp())/while
  889.1 83.4 %copy-start.34 = (f32[2,256,64]{1,0,2:T(2,128)}, f32[2,256,64]{1,0,2:T(2,128)S(1)}, u32[]{:S(2)}) copy-start(f32[2,256,64]{1,0,2:T(2,128)S(1)} %dynamic_update_slice.85) | copy-start | bytes 393220 | tf_op jit(solution)/shard_map/transpose(jvp())/while
  889.3 83.3 %copy-start.31 = (f32[2,256,64]{2,1,0:T(8,128)}, f32[2,256,64]{2,1,0:T(8,128)S(1)}, u32[]{:S(2)}) copy-start(f32[2,256,64]{2,1,0:T(8,128)S(1)} %bitcast_dynamic-update-slice_fusion.4) | copy-start | bytes 393220 | tf_op jit(solution)/shard_map/transpose(jvp())/while
  985.3 29.7 %copy-start.20 = (bf16[512,2048]{1,0:T(8,128)(2,1)S(1)}, bf16[512,2048]{1,0:T(8,128)(2,1)}, u32[]{:S(2)}) copy-start(bf16[512,2048]{1,0:T(8,128)(2,1)} %param.27) | copy-start | bytes 6291460
  985.3 29.7 %copy-start.49 = (f32[32,1,128]{2,1,0:T(1,128)S(1)}, f32[32,1,128]{2,1,0:T(1,128)}, u32[]{:S(2)}) copy-start(f32[32,1,128]{2,1,0:T(1,128)} %convert_element_type.115) | copy-start | bytes 49156
  985.3 29.8 %copy-start.56 = (f32[512]{0:T(512)S(1)}, f32[512]{0:T(512)}, u32[]{:S(2)}) copy-start(f32[512]{0:T(512)} %copy-done.55) | copy-start | bytes 6148
  985.3 29.8 %copy-start.64 = (f32[512]{0:T(512)S(1)}, f32[512]{0:T(512)}, u32[]{:S(2)}) copy-start(f32[512]{0:T(512)} %fusion.107) | copy-start | bytes 6148
  1015.0 481.4 %reduce-scatter.6.cloned.1.call-start = ((), (), s32[]{:S(2)}) async-start(), calls=%async_computation.5 | async-start | bytes 34603008 | tf_op jit(solution)/shard_map/reduce_scatter | solution.py:137
  1034.2 1203.6 %reduce-scatter.4.cloned.1.call-start = ((), (), s32[]{:S(2)}) async-start(), calls=%async_computation.4 | async-start | bytes 72450048 | tf_op jit(solution)/shard_map/reduce_scatter | solution.py:128
  1098.7 36.1 %copy-start.46 = (f32[4352]{0:T(1024)S(1)}, f32[4352]{0:T(1024)}, u32[]{:S(2)}) copy-start(f32[4352]{0:T(1024)} %get-tuple-element.720) | copy-start | bytes 52228
  1098.7 36.1 %copy-start.54 = (f32[4096]{0:T(1024)S(1)}, f32[4096]{0:T(1024)}, u32[]{:S(2)}) copy-start(f32[4096]{0:T(1024)} %get-tuple-element.718) | copy-start | bytes 49156
  1098.7 90.8 %copy-start.53 = (f32[512]{0:T(512)S(1)}, f32[512]{0:T(512)}, u32[]{:S(2)}) copy-start(f32[512]{0:T(512)} %copy-done.52) | copy-start | bytes 6148
  (52 other events, 373.4 us)
Sparse Core Ops, SparseCore 0:
  10.8 205.7 all-gather.4
  219.5 112.4 all-gather.6
  1015.1 118.5 all-reduce.32
  1136.4 359.8 reduce-scatter.5
  1499.2 738.5 reduce-scatter.3
where the time goes:
time: 2270 us; the launch traced here: 2240 us
  waiting for transfers between devices  1080 us (48%)
  local copies, waits for them, and re-layouts  530 us (23%)
  matrix products  264 us (12%)
  blocking collectives  197 us (9%)
  other arithmetic  158 us (7%)
    reduce_scatter x1, waiting for transfers between devices, settle_grads(): lax.psum_scatter(lax.dot_general(columns, proj_grad, (((0,), (0,)), ((),...  741 us
    dynamic_update_slice x12, local copies, waits for them, and re-layouts, ssd_mixer(): lax.scan(jax.checkpoint(partial(block_step, rounding=rounding)), zero_sta...  412 us
    reduce_scatter x1, waiting for transfers between devices, settle_grads(): lax.psum_scatter(lax.dot_general(columns, branch_grad, (((0,), (0,)), (()...  284 us
    unnamed x3, blocking collectives  116 us
    dot_general x6, matrix products, block_step(): jnp.einsum('hts,shp->thp', mixing, x_heads, preferred_element_type=jnp.fl...  72 us
    all_gather x1, waiting for transfers between devices, fetch_weights(): lax.all_gather(in_part, ('wide', 'narrow'), axis=0, tiled=True)  50.2 us
  transfers between devices with their start and end apart: 5, of which 3 were waited for; matrix products, arithmetic and copies ran while one was open for 22% of the time, Pallas kernels for 0%

commit v1 on v0

--- a/solution.py
+++ b/solution.py
@@ -128,20 +128,20 @@
     inw_own = lax.psum_scatter(
         lax.dot_general(
             columns, proj_grad, (((0,), (0,)), ((), ())), preferred_element_type=jnp.float32
-        ),
+        ).astype(jnp.bfloat16),
         ("wide", "narrow"),
         scatter_dimension=0,
         tiled=True,
-    )
+    ).astype(jnp.float32)
     columns = mixed_low
     outw_own = lax.psum_scatter(
         lax.dot_general(
             columns, branch_grad, (((0,), (0,)), ((), ())), preferred_element_type=jnp.float32
-        ),
+        ).astype(jnp.bfloat16),
         ("wide", "narrow"),
         scatter_dimension=0,
         tiled=True,
-    )
+    ).astype(jnp.float32)
     small_own = (
         lax.psum_scatter(norm_term, ("wide", "narrow"), scatter_dimension=0, tiled=True),
         lax.psum_scatter(conv_term, ("wide", "narrow"), scatter_dimension=0, tiled=True),

time: 2270 us -> 1740 us (0.77)
  waiting for transfers between devices: 1080 us -> 552 us
    reduce_scatter x1, waiting for transfers between devices: 741 us -> 376 us  [settle_grads(): lax.psum_scatter(lax.dot_general(columns, proj_grad, (((0,), (0,)), ((),...]
    reduce_scatter x1, waiting for transfers between devices: 284 us -> 125 us  [settle_grads(): lax.psum_scatter(lax.dot_general(columns, branch_grad, (((0,), (0,)), (()...]
  transfers between devices with their start and end apart: 5 -> 5, of which waited for: 3 -> 3; matrix products, arithmetic and copies ran while one was open for 22% -> 29% of each run, Pallas kernels for 0% -> 0%
where the time goes in v1:
time: 1740 us; the launch traced here: 1710 us
  waiting for transfers between devices  552 us (32%)
  local copies, waits for them, and re-layouts  530 us (30%)
  matrix products  256 us (15%)
  blocking collectives  190 us (11%)
  other arithmetic  162 us (9%)
    dynamic_update_slice x12, local copies, waits for them, and re-layouts, ssd_mixer(): lax.scan(jax.checkpoint(partial(block_step, rounding=rounding)), zero_sta...  412 us
    reduce_scatter x1, waiting for transfers between devices, settle_grads(): lax.psum_scatter(lax.dot_general(columns, proj_grad, (((0,), (0,)), ((),...  376 us
    reduce_scatter x1, waiting for transfers between devices, settle_grads(): lax.psum_scatter(lax.dot_general(columns, branch_grad, (((0,), (0,)), (()...  125 us
    unnamed x3, blocking collectives  109 us
    dot_general x6, matrix products, block_step(): jnp.einsum('hts,shp->thp', mixing, x_heads, preferred_element_type=jnp.fl...  71.9 us
    all_gather x1, waiting for transfers between devices, fetch_weights(): lax.all_gather(in_part, ('wide', 'narrow'), axis=0, tiled=True)  50 us
    all_gather x1, blocking collectives, fetch_weights(): lax.all_gather(gain_part, ('wide', 'narrow'), axis=0, tiled=True)  42.1 us
    all_gather x1, blocking collectives, fetch_weights(): lax.all_gather(conv_part, ('wide', 'narrow'), axis=0, tiled=True)  39 us
  transfers between devices with their start and end apart: 5, of which 3 were waited for; matrix products, arithmetic and copies ran while one was open for 29% of the time, Pallas kernels for 0%

profile of v1, /device:TPU:1, one launch (start us, length us, event | category | flops | bytes accessed | tf_op | source)
XLA Modules:
  0.0 1708.1 jit_solution(17202813251286906501)
XLA Ops:
  13.8 19.4 %all-reduce.29 = (f32[64]{0:T(128)S(1)}, f32[64]{0:T(128)S(1)}, f32[64]{0:T(128)S(1)}) all-reduce(f32[64]{0:T(128)S(1)} %dynamic-update-slice.1, f32[64]{0:T(128)S(1)} %dynamic-update-slice.2, f32[64]{0:T(128)S(1)} %dynamic-update-slice.4), channel_id=1, replica_groups=mesh['wide'=8,'narrow'=4] {'wide'}, use_global_device_ids=true, to_apply=%add.17 | all-reduce | flops 192 | bytes 1536
  35.4 45.5 %all-reduce.30 = (bf16[2048]{0:T(1024)(128)(2,1)S(1)}, bf16[4352]{0:T(1024)(128)(2,1)S(1)}) all-reduce(bf16[2048]{0:T(1024)(128)(2,1)S(1)} %dynamic-update-slice, bf16[4352]{0:T(1024)(128)(2,1)S(1)} %dynamic-update-slice.3), channel_id=1, replica_groups=mesh['wide'=8,'narrow'=4] {'wide','narrow'}, use_global_device_ids=true, to_apply=%add.16 | all-reduce | flops 6400 | bytes 25600
  81.0 42.1 %all-gather.1 = bf16[32,1,128]{2,1,0:T(2,128)(2,1)S(1)} all-gather(bf16[1,1,128]{2,1,0:T(2,128)(2,1)} %bitcast.427), channel_id=1, replica_groups=mesh['wide'=8,'narrow'=4] {'wide','narrow'}, dimensions={0}, use_global_device_ids=true | all-gather | bytes 8448 | tf_op jit(solution)/shard_map/all_gather | solution.py:101
  124.5 39.0 %all-gather = bf16[32,136,4]{1,2,0:T(4,128)(2,1)S(1)} all-gather(bf16[1,136,4]{1,2,0:T(4,128)(2,1)} %bitcast.426), channel_id=1, replica_groups=mesh['wide'=8,'narrow'=4] {'wide','narrow'}, dimensions={0}, use_global_device_ids=true | all-gather | bytes 35904 | tf_op jit(solution)/shard_map/all_gather | solution.py:99
  166.6 50.0 %all-gather.5.cloned.1.call-done = bf16[2048,8512]{1,0:T(8,128)(2,1)} async-done(((bf16[64,8512]{1,0:T(8,128)(2,1)}), bf16[2048,8512]{1,0:T(8,128)(2,1)}) %all-gather.5.cloned.1.call-update) | async-done | bytes 34865168 | tf_op jit(solution)/shard_map/all_gather | solution.py:96
  216.6 26.2 %fusion.100 = f32[512,8512]{0,1:T(8,128)} fusion(bf16[2048,8512]{1,0:T(8,128)(2,1)} %all-gather.5.cloned.1.call-done, bf16[512,2048]{1,0:T(8,128)(2,1)} %param.16, f32[2048]{0:T(1024)S(1)} %convert_element_type.107, f32[512]{0:T(512)S(1)} %fusion.106), kind=kOutput, calls=%fused_computation.183 | convolution fusion | flops 17855152128 | bytes 54405120 | tf_op jit(solution)/shard_map/dot_general | solution.py:182
  242.9 8.0 slice.132
  253.5 23.8 %fusion.81 = (f32[512,4352]{0,1:T(8,128)S(1)}, f32[512,4352]{0,1:T(8,128)}) fusion(f32[512,4352]{0,1:T(8,128)} %slice.132, f32[4352]{0:T(1024)S(1)} %get-tuple-element.725, f32[4352]{0:T(1024)S(1)} %get-tuple-element.726, f32[4352]{0:T(1024)S(1)} %get-tuple-element.727, f32[4352]{0:T(1024)S(1)} %get-tuple-element.724, f32[4352]{0:T(1024)S(1)} %convert_element_type.109), kind=kLoop, calls=%fused_computation.144 | loop fusion | flops 26738688 | bytes 26825728 | tf_op jit(solution)/shard_map/jvp(jit(silu))/mul | solution.py:66
  285.4 6.1 subtract_add_fusion.8
  297.4 5.5 broadcast.177.clone2
  302.9 257.0 %while.44 = (s32[]{:T(128)}, f32[64,128,64]{1,2,0:T(8,128)S(1)}, f32[2,256,4096]{1,0,2:T(2,128)}, f32[2,64,128,64]{2,3,1,0:T(8,128)}, f32[2,256,64]{1,2,0:T(8,12...) while((s32[]{:T(128)}, f32[64,128,64]{1,2,0:T(8,128)S(1)}, ...), condition=%wide.region_4.5_spmd.clone.clone, body=%wide.region_1.4_spmd.clone.clone.sunk | while | flops 1156104448 | bytes 122035080 | solution.py:78
  315.8 5.1 fusion.221
  320.9 8.1 bitcast_add_fusion.14
  329.0 19.2 %copy.361 = f32[1,256,4096]{1,0,2:T(1,128)} copy(f32[1,256,4096]{1,2,0:T(8,128)S(1)} %bitcast.404) | data formatting | bytes 8388608 | tf_op jit(solution)/shard_map/jvp()/while/body/jit(dynamic_update_index_in_dim)/dynamic_update_slice | solution.py:78
  348.2 83.3 %dynamic_update_slice.87 = f32[2,256,4096]{1,0,2:T(2,128)} dynamic-update-slice(f32[2,256,4096]{1,0,2:T(2,128)} %get-tuple-element.1047, f32[1,256,4096]{1,0,2:T(1,128)} %copy.361, s32[]{:T(128)S(6)} %copy.378, s32[]{:T(128)} %constant.121.clone.1..sunk.1, s32[]{:T(128)} %constant.121.clone.1..sunk.1) | dynamic-update-slice | bytes 8388612 | tf_op jit(solution)/shard_map/jvp()/while/body/jit(dynamic_update_index_in_dim)/dynamic_update_slice | solution.py:78
  444.0 5.1 fusion.221
  449.2 8.1 bitcast_add_fusion.14
  457.3 19.2 %copy.361 = f32[1,256,4096]{1,0,2:T(1,128)} copy(f32[1,256,4096]{1,2,0:T(8,128)S(1)} %bitcast.404) | data formatting | bytes 8388608 | tf_op jit(solution)/shard_map/jvp()/while/body/jit(dynamic_update_index_in_dim)/dynamic_update_slice | solution.py:78
  476.4 83.3 %dynamic_update_slice.87 = f32[2,256,4096]{1,0,2:T(2,128)} dynamic-update-slice(f32[2,256,4096]{1,0,2:T(2,128)} %get-tuple-element.1047, f32[1,256,4096]{1,0,2:T(1,128)} %copy.361, s32[]{:T(128)S(6)} %copy.378, s32[]{:T(128)} %constant.121.clone.1..sunk.1, s32[]{:T(128)} %constant.121.clone.1..sunk.1) | dynamic-update-slice | bytes 8388612 | tf_op jit(solution)/shard_map/jvp()/while/body/jit(dynamic_update_index_in_dim)/dynamic_update_slice | solution.py:78
  559.9 4.6 copy.296
  566.1 8.9 multiply_reduce_fusion.12
  575.1 17.8 %multiply_reduce_fusion.10 = (f32[4096]{0:T(1024)}, f32[512]{0:T(512)S(1)}, f32[512,4096]{0,1:T(8,128)}) fusion(f32[512,4096]{0,1:T(8,128)} %get-tuple-element.795, f32[512]{0:T(512)S(1)} %fusion.107, f32[4096]{0:T(1024)S(1)} %bitcast.422, bf16[4096,2048]{1,0:T(8,128)(2,1)} %all-gather.7.cloned.1.call-done, bf16[512,2048]{1,0:T(8,128)(2,1)S(1)} %copy-done.19, ...), kind=kOutput, calls=%fused_computation.150 | convolution fusion | flops 8605659136 | bytes 35690496 | tf_op jit(solution)/shard_map/dot_general | solution.py:205
  592.9 18.1 %multiply_reduce_fusion.9 = (f32[4096]{0:T(1024)}, f32[512,4096]{0,1:T(8,128)}, f32[512,4096]{0,1:T(8,128)}) fusion(f32[512,4096]{0,1:T(8,128)} %copy-done.2, f32[512,8512]{0,1:T(8,128)} %fusion.100, f32[512,4096]{0,1:T(8,128)} %get-tuple-element.795, f32[512]{0:T(512)S(1)} %multiply_multiply_fusion.4, f32[512]{0:T(512)S(1)} %fusion.107, ...), kind=kLoop, calls=%fused_computation.149 | loop fusion | flops 44036096 | bytes 58773504 | tf_op jit(solution)/shard_map/transpose(jvp())/reduce_sum | solution.py:89
  611.0 10.5 reshape.410
  624.4 5.4 broadcast.177.clone
  629.8 342.9 %while.43 = (s32[]{:T(128)}, f32[64,128,64]{1,2,0:T(8,128)}, f32[2,256,4096]{1,0,2:T(2,128)}, f32[2,256,128]{2,1,0:T(8,128)}, f32[2,256,128]{2,1,0:T(8,128)}, /*...) while((s32[]{:T(128)}, f32[64,128,64]{1,2,0:T(8,128)}, ...), condition=%wide.region_19.20_spmd.clone, body=%wide.region_7.19_spmd.clone.sunk | while | flops 2587640576 | bytes 238366704 | solution.py:78
  651.8 5.0 multiply_reduce_fusion.18
  657.0 16.5 fusion.205
  677.6 11.4 bitcast_add_fusion.12
  693.3 19.1 %copy.353 = f32[1,256,4096]{1,0,2:T(1,128)} copy(f32[1,256,4096]{1,2,0:T(8,128)S(1)} %bitcast.402) | data formatting | bytes 8388608 | tf_op jit(solution)/shard_map/transpose(jvp())/while/body/jit(dynamic_update_index_in_dim)/dynamic_update_slice | solution.py:78
  716.9 83.3 %dynamic_update_slice.84 = f32[2,256,4096]{1,0,2:T(2,128)} dynamic-update-slice(f32[2,256,4096]{1,0,2:T(2,128)} %get-tuple-element.1090, f32[1,256,4096]{1,0,2:T(1,128)} %copy.353, s32[]{:T(128)S(6)} %sub.332, s32[]{:T(128)} %constant.121.clone.1..sunk, s32[]{:T(128)} %constant.121.clone.1..sunk) | dynamic-update-slice | bytes 8388612 | tf_op jit(solution)/shard_map/transpose(jvp())/while/body/jit(dynamic_update_index_in_dim)/dynamic_update_slice | solution.py:78
  824.1 5.0 multiply_reduce_fusion.18
  829.4 16.5 fusion.205
  849.9 11.4 bitcast_add_fusion.12
  865.6 19.1 %copy.353 = f32[1,256,4096]{1,0,2:T(1,128)} copy(f32[1,256,4096]{1,2,0:T(8,128)S(1)} %bitcast.402) | data formatting | bytes 8388608 | tf_op jit(solution)/shard_map/transpose(jvp())/while/body/jit(dynamic_update_index_in_dim)/dynamic_update_slice | solution.py:78
  889.2 83.3 %dynamic_update_slice.84 = f32[2,256,4096]{1,0,2:T(2,128)} dynamic-update-slice(f32[2,256,4096]{1,0,2:T(2,128)} %get-tuple-element.1090, f32[1,256,4096]{1,0,2:T(1,128)} %copy.353, s32[]{:T(128)S(6)} %sub.332, s32[]{:T(128)} %constant.121.clone.1..sunk, s32[]{:T(128)} %constant.121.clone.1..sunk) | dynamic-update-slice | bytes 8388612 | tf_op jit(solution)/shard_map/transpose(jvp())/while/body/jit(dynamic_update_index_in_dim)/dynamic_update_slice | solution.py:78
  979.3 6.0 multiply_add_fusion.1
  985.3 27.8 %multiply_reduce_fusion.7 = (f32[4352]{0:T(1024)S(1)}, f32[4352]{0:T(1024)S(1)}, f32[4352]{0:T(1024)S(1)}, f32[4352]{0:T(1024)S(1)}, f32[4352]{0:T(1024)S(1)}, /*index=5*/f32[512,4352]{0,1:T(8,128)}) fusion(f32[512,4352]{0,1:T(8,128)} %slice.132, f32[512,8512]{0,1:T(8,128)} %fusion.100, f32[512,4352]{0,1:T(8,128)} %get-tuple-element.797, ...), kind=kLoop, calls=%fused_computation.141 | loop fusion | flops 44542720 | bytes 44651520 | tf_op jit(solution)/shard_map/transpose(jvp())/reduce_sum | solution.py:65
  1014.0 16.3 convolution_convert_fusion.1
  1032.6 12.4 broadcast_multiply_fusion
  1045.0 14.4 pad_add_fusion
  1059.4 28.2 %convolution_convert_fusion = bf16[2048,8512]{1,0:T(8,128)(2,1)} fusion(bf16[512,2048]{1,0:T(8,128)(2,1)S(1)} %copy-done.13, f32[2048]{0:T(1024)S(1)} %copy-done.50, f32[512]{0:T(512)S(1)} %copy-done.57, f32[512,4096]{0,1:T(8,128)} %get-tuple-element.814, f32[512,4352]{0,1:T(8,128)} %pad_add_fusion, f32[512,64]{0,1:T(8,128)S(1)} %get-tuple-element.792), kind=kOutput, calls=%fused_computation.124 | convolution fusion | flops 17885659136 | bytes 54405120 | tf_op jit(solution)/shard_map/dot_general | solution.py:129
  1089.2 36.0 %fusion.88 = (f32[2048]{0:T(1024)S(1)}, f32[512]{0:T(512)S(1)}, f32[512,2048]{1,0:T(8,128)}) fusion(bf16[512,2048]{1,0:T(8,128)(2,1)S(1)} %copy-done.13, f32[512]{0:T(512)S(1)} %copy-done.57, f32[2048]{0:T(1024)S(1)} %copy-done.50, bf16[2048,8512]{1,0:T(8,128)(2,1)} %all-gather.5.cloned.1.call-done, f32[512,4096]{0,1:T(8,128)} %get-tuple-element.814, ...), kind=kOutput, calls=%fused_computation.174 | convolution fusion | flops 17871370240 | bytes 58609664 | tf_op jit(solution)/shard_map/dot_general | solution.py:210
  1125.2 43.6 %all-reduce.28 = (f32[2048]{0:T(1024)S(1)}, f32[4352]{0:T(1024)S(1)}, f32[4096]{0:T(1024)S(1)}, f32[256]{0:T(256)S(1)}, f32[256]{0:T(256)S(1)}, /*index=5*/f32[256]{0:T(256)S(1)}) all-reduce(f32[2048]{0:T(1024)S(1)} %get-tuple-element.722, ...), channel_id=4, replica_groups=mesh['wide'=8,'narrow'=4] {'wide','narrow'}, use_global_device_ids=true, to_apply=%region_24.25.clone | all-reduce | flops 11264 | bytes 90112
  1172.3 5.6 fusion.90
  1177.9 16.2 fusion.92
  1195.5 125.1 %reduce-scatter.6.cloned.1.call-done = bf16[128,2048]{1,0:T(8,128)(2,1)} async-done(((bf16[4096,2048]{1,0:T(8,128)(2,1)}), bf16[128,2048]{1,0:T(8,128)(2,1)}) %reduce-scatter.6.cloned.1.call-update) | async-done | bytes 524304 | tf_op jit(solution)/shard_map/reduce_scatter | solution.py:137
  1322.7 375.7 %reduce-scatter.4.cloned.1.call-done = bf16[64,8512]{1,0:T(8,128)(2,1)} async-done(((bf16[2048,8512]{1,0:T(8,128)(2,1)}), bf16[64,8512]{1,0:T(8,128)(2,1)}) %reduce-scatter.4.cloned.1.call-update) | async-done | bytes 1089552 | tf_op jit(solution)/shard_map/reduce_scatter | solution.py:128
  (397 shorter events, 149.3 us)
Async XLA Ops:
  7.2 209.5 %all-gather.5.cloned.1.call-start = ((), (), s32[]{:S(2)}) async-start(), calls=%async_computation.2 | async-start | bytes 36225024 | tf_op jit(solution)/shard_map/all_gather | solution.py:96
  7.9 567.1 %all-gather.7.cloned.1.call-start = ((), (), s32[]{:S(2)}) async-start(), calls=%async_computation.3 | async-start | bytes 17301504 | tf_op jit(solution)/shard_map/all_gather | solution.py:97
  8.7 1185.4 %all-reduce.33.cloned.1.call-start = ((), (), s32[]{:S(2)}) async-start(), calls=%async_computation.6 | async-start | bytes 139264
  33.3 217.7 %copy-start.58 = (f32[64]{0:T(128)}, f32[64]{0:T(128)S(1)}, u32[]{:S(2)}) copy-start(f32[64]{0:T(128)S(1)} %get-tuple-element.782) | copy-start | bytes 772
  33.3 217.7 %copy-start.60 = (f32[64]{0:T(128)}, f32[64]{0:T(128)S(1)}, u32[]{:S(2)}) copy-start(f32[64]{0:T(128)S(1)} %exp.80) | copy-start | bytes 772
  81.0 161.9 %copy-start.49 = (f32[2048]{0:T(1024)}, f32[2048]{0:T(1024)S(1)}, u32[]{:S(2)}) copy-start(f32[2048]{0:T(1024)S(1)} %convert_element_type.107) | copy-start | bytes 24580
  164.5 89.0 %copy-start.38 = (f32[4352]{0:T(1024)}, f32[4352]{0:T(1024)S(1)}, u32[]{:S(2)}) copy-start(f32[4352]{0:T(1024)S(1)} %get-tuple-element.724) | copy-start | bytes 52228
  164.5 89.0 %copy-start.40 = (f32[4352]{0:T(1024)}, f32[4352]{0:T(1024)S(1)}, u32[]{:S(2)}) copy-start(f32[4352]{0:T(1024)S(1)} %get-tuple-element.725) | copy-start | bytes 52228
  164.5 89.0 %copy-start.42 = (f32[4352]{0:T(1024)}, f32[4352]{0:T(1024)S(1)}, u32[]{:S(2)}) copy-start(f32[4352]{0:T(1024)S(1)} %get-tuple-element.726) | copy-start | bytes 52228
  164.5 89.0 %copy-start.44 = (f32[4352]{0:T(1024)}, f32[4352]{0:T(1024)S(1)}, u32[]{:S(2)}) copy-start(f32[4352]{0:T(1024)S(1)} %get-tuple-element.727) | copy-start | bytes 52228
  166.6 76.3 %copy-start.51 = (f32[512]{0:T(512)}, f32[512]{0:T(512)S(1)}, u32[]{:S(2)}) copy-start(f32[512]{0:T(512)S(1)} %fusion.91) | copy-start | bytes 6148
  166.6 76.3 %copy-start.56 = (f32[512]{0:T(512)}, f32[512]{0:T(512)S(1)}, u32[]{:S(2)}) copy-start(f32[512]{0:T(512)S(1)} %fusion.106) | copy-start | bytes 6148
  252.0 25.3 %copy-start.24 = (f32[512,64]{0,1:T(8,128)}, f32[512,64]{0,1:T(8,128)S(1)}, u32[]{:S(2)}) copy-start(f32[512,64]{0,1:T(8,128)S(1)} %get-tuple-element.799) | copy-start | bytes 393220
  348.2 83.3 %copy-start.8 = (f32[64,128,64]{1,2,0:T(8,128)S(1)}, f32[64,128,64]{1,2,0:T(8,128)}, u32[]{:S(2)}) copy-start(f32[64,128,64]{1,2,0:T(8,128)} %bitcast_add_fusion.13) | copy-start | bytes 6291460 | tf_op jit(solution)/shard_map/jvp()/while
  348.2 83.3 %copy-start.18 = (pred[256,256]{1,0:T(8,128)(4,1)S(1)}, pred[256,256]{1,0:T(8,128)(4,1)}, u32[]{:S(2)}) copy-start(pred[256,256]{1,0:T(8,128)(4,1)} %copy-done.17) | copy-start | bytes 196612 | tf_op jit(solution)/shard_map/jvp()/while
  476.4 83.3 %copy-start.8 = (f32[64,128,64]{1,2,0:T(8,128)S(1)}, f32[64,128,64]{1,2,0:T(8,128)}, u32[]{:S(2)}) copy-start(f32[64,128,64]{1,2,0:T(8,128)} %bitcast_add_fusion.13) | copy-start | bytes 6291460 | tf_op jit(solution)/shard_map/jvp()/while
  476.4 83.3 %copy-start.18 = (pred[256,256]{1,0:T(8,128)(4,1)S(1)}, pred[256,256]{1,0:T(8,128)(4,1)}, u32[]{:S(2)}) copy-start(pred[256,256]{1,0:T(8,128)(4,1)} %copy-done.17) | copy-start | bytes 196612 | tf_op jit(solution)/shard_map/jvp()/while
  575.0 17.9 %copy-start.54 = (f32[512]{0:T(512)}, f32[512]{0:T(512)S(1)}, u32[]{:S(2)}) copy-start(f32[512]{0:T(512)S(1)} %fusion.107) | copy-start | bytes 6148
  630.2 26.8 %copy-start.23 = (pred[256,256]{1,0:T(8,128)(4,1)}, pred[256,256]{1,0:T(8,128)(4,1)S(1)}, u32[]{:S(2)}) copy-start(pred[256,256]{1,0:T(8,128)(4,1)S(1)} %iota_compare_fusion.4) | copy-start | bytes 196612 | tf_op jit(solution)/shard_map/transpose(jvp())/while
  651.8 21.7 %copy-start.16 = (f32[256,256]{1,0:T(8,128)}, f32[256,256]{1,0:T(8,128)S(1)}, u32[]{:S(2)}) copy-start(f32[256,256]{1,0:T(8,128)S(1)} %fusion.204) | copy-start | bytes 786436 | tf_op jit(solution)/shard_map/transpose(jvp())/while
  691.2 21.2 %copy-start.28 = (f32[2,256,128]{2,1,0:T(8,128)S(1)}, f32[2,256,128]{2,1,0:T(8,128)}, u32[]{:S(2)}) copy-start(f32[2,256,128]{2,1,0:T(8,128)} %get-tuple-element.1091) | copy-start | bytes 786436 | tf_op jit(solution)/shard_map/transpose(jvp())/while
  691.2 21.5 %copy-start.26 = (f32[2,256,128]{2,1,0:T(8,128)S(1)}, f32[2,256,128]{2,1,0:T(8,128)}, u32[]{:S(2)}) copy-start(f32[2,256,128]{2,1,0:T(8,128)} %get-tuple-element.1092) | copy-start | bytes 786436 | tf_op jit(solution)/shard_map/transpose(jvp())/while
  691.2 25.5 %copy-start.21 = (f32[64,256]{1,0:T(8,128)S(1)}, f32[64,256]{1,0:T(8,128)}, u32[]{:S(2)}) copy-start(f32[64,256]{1,0:T(8,128)} %get-tuple-element.1014) | copy-start | bytes 196612 | tf_op jit(solution)/shard_map/transpose(jvp())/while
  693.3 22.5 %copy-start.33 = (f32[2,256,64]{1,0,2:T(2,128)S(1)}, f32[2,256,64]{1,0,2:T(2,128)}, u32[]{:S(2)}) copy-start(f32[2,256,64]{1,0,2:T(2,128)} %get-tuple-element.1094) | copy-start | bytes 393220 | tf_op jit(solution)/shard_map/transpose(jvp())/while
  693.3 23.5 %copy-start.30 = (f32[2,256,64]{2,1,0:T(8,128)S(1)}, f32[2,256,64]{2,1,0:T(8,128)}, u32[]{:S(2)}) copy-start(f32[2,256,64]{2,1,0:T(8,128)} %get-tuple-element.1093) | copy-start | bytes 393220 | tf_op jit(solution)/shard_map/transpose(jvp())/while
  712.7 87.5 %copy-start.29 = (f32[2,256,128]{2,1,0:T(8,128)}, f32[2,256,128]{2,1,0:T(8,128)S(1)}, u32[]{:S(2)}) copy-start(f32[2,256,128]{2,1,0:T(8,128)S(1)} %fusion.209) | copy-start | bytes 786436 | tf_op jit(solution)/shard_map/transpose(jvp())/while
  712.9 87.3 %copy-start.27 = (f32[2,256,128]{2,1,0:T(8,128)}, f32[2,256,128]{2,1,0:T(8,128)S(1)}, u32[]{:S(2)}) copy-start(f32[2,256,128]{2,1,0:T(8,128)S(1)} %fusion.211) | copy-start | bytes 786436 | tf_op jit(solution)/shard_map/transpose(jvp())/while
  716.7 83.4 %copy-start.34 = (f32[2,256,64]{1,0,2:T(2,128)}, f32[2,256,64]{1,0,2:T(2,128)S(1)}, u32[]{:S(2)}) copy-start(f32[2,256,64]{1,0,2:T(2,128)S(1)} %dynamic_update_slice.85) | copy-start | bytes 393220 | tf_op jit(solution)/shard_map/transpose(jvp())/while
  716.9 83.3 %copy-start.31 = (f32[2,256,64]{2,1,0:T(8,128)}, f32[2,256,64]{2,1,0:T(8,128)S(1)}, u32[]{:S(2)}) copy-start(f32[2,256,64]{2,1,0:T(8,128)S(1)} %bitcast_dynamic-update-slice_fusion.4) | copy-start | bytes 393220 | tf_op jit(solution)/shard_map/transpose(jvp())/while
  800.2 29.1 %copy-start.23 = (pred[256,256]{1,0:T(8,128)(4,1)}, pred[256,256]{1,0:T(8,128)(4,1)S(1)}, u32[]{:S(2)}) copy-start(pred[256,256]{1,0:T(8,128)(4,1)S(1)} %iota_compare_fusion.4) | copy-start | bytes 196612 | tf_op jit(solution)/shard_map/transpose(jvp())/while
  824.1 21.7 %copy-start.16 = (f32[256,256]{1,0:T(8,128)}, f32[256,256]{1,0:T(8,128)S(1)}, u32[]{:S(2)}) copy-start(f32[256,256]{1,0:T(8,128)S(1)} %fusion.204) | copy-start | bytes 786436 | tf_op jit(solution)/shard_map/transpose(jvp())/while
  863.5 21.2 %copy-start.28 = (f32[2,256,128]{2,1,0:T(8,128)S(1)}, f32[2,256,128]{2,1,0:T(8,128)}, u32[]{:S(2)}) copy-start(f32[2,256,128]{2,1,0:T(8,128)} %get-tuple-element.1091) | copy-start | bytes 786436 | tf_op jit(solution)/shard_map/transpose(jvp())/while
  863.5 21.5 %copy-start.26 = (f32[2,256,128]{2,1,0:T(8,128)S(1)}, f32[2,256,128]{2,1,0:T(8,128)}, u32[]{:S(2)}) copy-start(f32[2,256,128]{2,1,0:T(8,128)} %get-tuple-element.1092) | copy-start | bytes 786436 | tf_op jit(solution)/shard_map/transpose(jvp())/while
  863.5 25.5 %copy-start.21 = (f32[64,256]{1,0:T(8,128)S(1)}, f32[64,256]{1,0:T(8,128)}, u32[]{:S(2)}) copy-start(f32[64,256]{1,0:T(8,128)} %get-tuple-element.1014) | copy-start | bytes 196612 | tf_op jit(solution)/shard_map/transpose(jvp())/while
  865.6 22.5 %copy-start.33 = (f32[2,256,64]{1,0,2:T(2,128)S(1)}, f32[2,256,64]{1,0,2:T(2,128)}, u32[]{:S(2)}) copy-start(f32[2,256,64]{1,0,2:T(2,128)} %get-tuple-element.1094) | copy-start | bytes 393220 | tf_op jit(solution)/shard_map/transpose(jvp())/while
  865.6 23.5 %copy-start.30 = (f32[2,256,64]{2,1,0:T(8,128)S(1)}, f32[2,256,64]{2,1,0:T(8,128)}, u32[]{:S(2)}) copy-start(f32[2,256,64]{2,1,0:T(8,128)} %get-tuple-element.1093) | copy-start | bytes 393220 | tf_op jit(solution)/shard_map/transpose(jvp())/while
  885.0 87.5 %copy-start.29 = (f32[2,256,128]{2,1,0:T(8,128)}, f32[2,256,128]{2,1,0:T(8,128)S(1)}, u32[]{:S(2)}) copy-start(f32[2,256,128]{2,1,0:T(8,128)S(1)} %fusion.209) | copy-start | bytes 786436 | tf_op jit(solution)/shard_map/transpose(jvp())/while
  885.2 87.3 %copy-start.27 = (f32[2,256,128]{2,1,0:T(8,128)}, f32[2,256,128]{2,1,0:T(8,128)S(1)}, u32[]{:S(2)}) copy-start(f32[2,256,128]{2,1,0:T(8,128)S(1)} %fusion.211) | copy-start | bytes 786436 | tf_op jit(solution)/shard_map/transpose(jvp())/while
  889.1 83.4 %copy-start.34 = (f32[2,256,64]{1,0,2:T(2,128)}, f32[2,256,64]{1,0,2:T(2,128)S(1)}, u32[]{:S(2)}) copy-start(f32[2,256,64]{1,0,2:T(2,128)S(1)} %dynamic_update_slice.85) | copy-start | bytes 393220 | tf_op jit(solution)/shard_map/transpose(jvp())/while
  889.2 83.3 %copy-start.31 = (f32[2,256,64]{2,1,0:T(8,128)}, f32[2,256,64]{2,1,0:T(8,128)S(1)}, u32[]{:S(2)}) copy-start(f32[2,256,64]{2,1,0:T(8,128)S(1)} %bitcast_dynamic-update-slice_fusion.4) | copy-start | bytes 393220 | tf_op jit(solution)/shard_map/transpose(jvp())/while
  985.3 28.7 %copy-start.20 = (bf16[512,2048]{1,0:T(8,128)(2,1)S(1)}, bf16[512,2048]{1,0:T(8,128)(2,1)}, u32[]{:S(2)}) copy-start(bf16[512,2048]{1,0:T(8,128)(2,1)} %param.27) | copy-start | bytes 6291460
  985.3 28.7 %copy-start.48 = (f32[32,1,128]{2,1,0:T(1,128)S(1)}, f32[32,1,128]{2,1,0:T(1,128)}, u32[]{:S(2)}) copy-start(f32[32,1,128]{2,1,0:T(1,128)} %convert_element_type.131) | copy-start | bytes 49156
  985.3 28.7 %copy-start.55 = (f32[512]{0:T(512)S(1)}, f32[512]{0:T(512)}, u32[]{:S(2)}) copy-start(f32[512]{0:T(512)} %copy-done.54) | copy-start | bytes 6148
  985.3 28.7 %copy-start.63 = (f32[512]{0:T(512)S(1)}, f32[512]{0:T(512)}, u32[]{:S(2)}) copy-start(f32[512]{0:T(512)} %fusion.105) | copy-start | bytes 6148
  1013.9 306.7 %reduce-scatter.6.cloned.1.call-start = ((), (), s32[]{:S(2)}) async-start(), calls=%async_computation.5 | async-start | bytes 17301504 | tf_op jit(solution)/shard_map/reduce_scatter | solution.py:137
  1030.4 668.0 %reduce-scatter.4.cloned.1.call-start = ((), (), s32[]{:S(2)}) async-start(), calls=%async_computation.4 | async-start | bytes 36225024 | tf_op jit(solution)/shard_map/reduce_scatter | solution.py:128
  1089.1 36.0 %copy-start.53 = (f32[4096]{0:T(1024)S(1)}, f32[4096]{0:T(1024)}, u32[]{:S(2)}) copy-start(f32[4096]{0:T(1024)} %get-tuple-element.718) | copy-start | bytes 49156
  1089.2 83.1 %copy-start.52 = (f32[512]{0:T(512)S(1)}, f32[512]{0:T(512)}, u32[]{:S(2)}) copy-start(f32[512]{0:T(512)} %copy-done.51) | copy-start | bytes 6148
  (51 other events, 354.6 us)
Sparse Core Ops, SparseCore 0:
  10.8 205.7 all-gather.4
  219.5 112.4 all-gather.6
  1014.0 119.0 all-reduce.32
  1135.3 185.2 reduce-scatter.5
  1322.7 375.5 reduce-scatter.3

commit v2 on v1

v2 whole, which is shorter than its diff:
```python
import jax
import jax.numpy as jnp
from jax import lax
from jax.experimental import pallas as pl
from jax.experimental.pallas import tpu as pltpu
from jax.sharding import PartitionSpec as P

HEADS = 64
HEAD_DIM = 64
NSTATE = 128
KCONV = 4
DIN = HEADS * HEAD_DIM
CHUNK = 128
GROUP = 256
NEVER = -1e30


EPS = 1e-05


def silu_parts(values):
    gate = 1.0 / (1.0 + jnp.exp(-values))
    return gate, values * gate


def mm(left, right):
    return lax.dot_general(left, right, (((1,), (0,)), ((), ())), preferred_element_type=jnp.float32)


def mm_nt(left, right):
    return lax.dot_general(left, right, (((1,), (1,)), ((), ())), preferred_element_type=jnp.float32)


def mm_tn(left, right):
    return lax.dot_general(left, right, (((0,), (0,)), ((), ())), preferred_element_type=jnp.float32)


def low16(values):
    return values.astype(jnp.bfloat16)


def tile_masks():
    row_id = lax.broadcasted_iota(jnp.int32, (CHUNK, CHUNK), 0)
    col_id = lax.broadcasted_iota(jnp.int32, (CHUNK, CHUNK), 1)
    return row_id >= col_id, col_id < HEAD_DIM


def conv_tile(pad_ref, par_ref, start, lanes):
    total = par_ref[4:5, lanes]
    for tap in range(KCONV):
        first = start + 8 - (KCONV - 1) + tap
        total = total + pad_ref[first : first + CHUNK, lanes] * par_ref[tap : tap + 1, lanes]
    return total


def fill_pad(pad_ref, source_ref):
    pad_ref[0:8, :] = jnp.zeros((8, GROUP), jnp.float32)
    pad_ref[8:, :] = source_ref[...]


def ssd_forward_kernel(
    xin_ref, z_ref, par_ref, b_ref, c_ref, bt_ref, dtc_ref, cumc_ref, dtr_ref, cumr_ref,
    x_ref, y_ref, s_ref, ssq_ref, pad_ref,
):
    rows = xin_ref.shape[0]
    causal, first_head = tile_masks()
    fill_pad(pad_ref, xin_ref)

    @pl.when(pl.program_id(1) == 0)
    def _():
        ssq_ref[...] = jnp.zeros(ssq_ref.shape, jnp.float32)

    for pair in range(GROUP // 128):
        lanes = slice(pair * 128, pair * 128 + 128)
        state = None
        for q in range(rows // CHUNK):
            span = slice(q * CHUNK, q * CHUNK + CHUNK)
            c_dot_b = mm_nt(c_ref[span, :], b_ref[span, :])
            _, active = silu_parts(conv_tile(pad_ref, par_ref, q * CHUNK, lanes))
            x_low = low16(active)
            x_ref[span, lanes] = x_low
            x_wide = x_low.astype(jnp.float32)
            within, cums, dts, ends = [], [], [], []
            for sub in range(2):
                head = pair * 2 + sub
                col = cumc_ref[0, span, head : head + 1]
                row = cumr_ref[0, head : head + 1, span]
                dt_row = dtr_ref[0, head : head + 1, span]
                decay = jnp.exp(jnp.where(causal, col - row, NEVER))
                within.append(mm(low16(c_dot_b * decay * dt_row), x_low))
                cums.append(col)
                dts.append(dtc_ref[0, span, head : head + 1])
                ends.append(cumc_ref[0, q * CHUNK + CHUNK - 1 : q * CHUNK + CHUNK, head : head + 1])
            out = jnp.where(first_head, within[0], within[1]) + par_ref[5:6, lanes] * x_wide
            if q:
                s_ref[q - 1, :, lanes] = low16(state)
                entry = jnp.where(first_head, jnp.exp(cums[0]), jnp.exp(cums[1]))
                out = out + entry * mm(c_ref[span, :], low16(state))
            y_ref[span, lanes] = out
            _, gate = silu_parts(z_ref[span, lanes])
            gated = out * gate
            ssq_ref[span, :] += gated * gated
            if q + 1 < rows // CHUNK:
                weight = jnp.where(
                    first_head, jnp.exp(ends[0] - cums[0]) * dts[0], jnp.exp(ends[1] - cums[1]) * dts[1]
                )
                fresh = mm(bt_ref[:, span], low16(x_wide * weight))
                if q:
                    fresh = fresh + state * jnp.where(first_head, jnp.exp(ends[0]), jnp.exp(ends[1]))
                state = fresh


def ssd_backward_kernel(
    xin_ref, z_ref, par_ref, b_ref, c_ref, ct_ref, dtc_ref, cumc_ref, dtr_ref, cumr_ref,
    x_ref, y_ref, s_ref, mg_ref, rc_ref,
    zg_ref, xg_ref, pg_ref, gb_ref, gc_ref, rv_ref, u_ref, e_ref,
    pad_ref, gpad_ref, gcb_ref,
):
    rows = xin_ref.shape[0]
    count = rows // CHUNK
    causal, first_head = tile_masks()
    lane_id = lax.broadcasted_iota(jnp.int32, (CHUNK, 128), 1)
    fill_pad(pad_ref, xin_ref)
    gpad_ref[rows:, :] = jnp.zeros((8, GROUP), jnp.float32)

    @pl.when(pl.program_id(1) == 0)
    def _():
        gb_ref[...] = jnp.zeros(gb_ref.shape, jnp.float32)
        gc_ref[...] = jnp.zeros(gc_ref.shape, jnp.float32)
        gcb_ref[...] = jnp.zeros(gcb_ref.shape, jnp.float32)

    columns = [jnp.zeros((CHUNK, 128), jnp.float32) for _ in range(count)]
    for pair in range(GROUP // 128):
        lanes = slice(pair * 128, pair * 128 + 128)
        state_grad = None
        sums = [jnp.zeros((1, 128), jnp.float32) for _ in range(7)]
        for q in reversed(range(count)):
            span = slice(q * CHUNK, q * CHUNK + CHUNK)
            b_low, c_low = b_ref[span, :], c_ref[span, :]
            c_dot_b = mm_nt(c_low, b_low)
            z_tile, y_tile, mg_tile = z_ref[span, lanes], y_ref[span, lanes], mg_ref[span, lanes]
            scale, coef = rc_ref[span, 0:1], rc_ref[span, 1:2]
            gate_sig, gate = silu_parts(z_tile)
            gated = y_tile * gate
            scaled = scale * mg_tile
            gated_grad = scaled * par_ref[6:7, lanes] - gated * coef
            zg_ref[span, lanes] = low16(
                gated_grad * y_tile * (gate_sig * (1.0 + z_tile * (1.0 - gate_sig)))
            )
            grad = gated_grad * gate
            grad_low = low16(grad)
            x_low = x_ref[span, lanes]
            x_wide = x_low.astype(jnp.float32)
            sums[6] += jnp.sum(gated * scaled, axis=0, keepdims=True)
            sums[5] += jnp.sum(grad * x_wide, axis=0, keepdims=True)
            cums, ends = [], []
            for sub in range(2):
                head = pair * 2 + sub
                cums.append(cumc_ref[0, span, head : head + 1])
                ends.append(cumc_ref[0, q * CHUNK + CHUNK - 1 : q * CHUNK + CHUNK, head : head + 1])
            entry = jnp.where(first_head, jnp.exp(cums[0]), jnp.exp(cums[1]))
            carried = jnp.zeros((CHUNK, 128), jnp.float32)
            entered = low16(grad * entry)
            if q:
                s_low = s_ref[q - 1, :, lanes]
                carried = grad * entry * mm(c_low, s_low)
                gc_ref[span, :] += mm_nt(entered, s_low)
            x_grad = par_ref[5:6, lanes] * grad
            leaving = None
            if state_grad is not None:
                sg_low = low16(state_grad)
                late = jnp.where(first_head, jnp.exp(ends[0] - cums[0]), jnp.exp(ends[1] - cums[1]))
                dt_cols = [dtc_ref[0, span, pair * 2 + sub : pair * 2 + sub + 1] for sub in range(2)]
                weight = late * jnp.where(first_head, dt_cols[0], dt_cols[1])
                b_state = mm(b_low, sg_low)
                x_grad = x_grad + weight * b_state
                leaving = late * x_wide * b_state
                gb_ref[span, :] += mm_nt(low16(x_wide * weight), sg_low)
            for sub in range(2):
                head = pair * 2 + sub
                mine = first_head if sub == 0 else jnp.logical_not(first_head)
                row = cumr_ref[0, head : head + 1, span]
                dt_row = dtr_ref[0, head : head + 1, span]
                decay = jnp.exp(jnp.where(causal, cums[sub] - row, NEVER))
                grad_mine = jnp.where(mine, grad_low, jnp.zeros_like(grad_low))
                mix_grad = mm_nt(grad_mine, x_low) * decay
                x_grad = x_grad + mm_tn(low16(c_dot_b * decay * dt_row), grad_mine)
                gcb_ref[span, :] += mix_grad * dt_row
                direct = mix_grad * c_dot_b
                u_ref[0, head : head + 1, span] = jnp.sum(direct, axis=0, keepdims=True)
                total = direct * dt_row + jnp.where(mine, carried, 0.0)
                columns[q] = jnp.where(
                    lane_id == head, jnp.sum(total, axis=1, keepdims=True), columns[q]
                )
                if leaving is not None:
                    columns[q] = jnp.where(
                        lane_id == head + GROUP // HEAD_DIM,
                        jnp.sum(jnp.where(mine, leaving, 0.0), axis=1, keepdims=True),
                        columns[q],
                    )
            pre = conv_tile(pad_ref, par_ref, q * CHUNK, lanes)
            pre_sig, _ = silu_parts(pre)
            pre_grad = x_grad * (pre_sig * (1.0 + pre * (1.0 - pre_sig)))
            gpad_ref[span, lanes] = pre_grad
            sums[4] += jnp.sum(pre_grad, axis=0, keepdims=True)
            back = jnp.zeros((CHUNK, 128), jnp.float32)
            for tap in range(KCONV):
                first = q * CHUNK + 8 - (KCONV - 1) + tap
                sums[tap] += jnp.sum(pre_grad * pad_ref[first : first + CHUNK, lanes], axis=0, keepdims=True)
                ahead = q * CHUNK + KCONV - 1 - tap
                back = back + gpad_ref[ahead : ahead + CHUNK, lanes] * par_ref[tap : tap + 1, lanes]
            xg_ref[span, lanes] = low16(back)
            end_scale = jnp.where(first_head, jnp.exp(ends[0]), jnp.exp(ends[1]))[0:1, :]
            if q and state_grad is not None:
                e_ref[0, q : q + 1, lanes] = end_scale * jnp.sum(
                    s_low.astype(jnp.float32) * state_grad, axis=0, keepdims=True
                )
            else:
                e_ref[0, q : q + 1, lanes] = jnp.zeros((1, 128), jnp.float32)
            if q:
                fresh = mm(ct_ref[:, span], entered)
                state_grad = fresh if state_grad is None else fresh + end_scale * state_grad
        for index in range(7):
            pg_ref[0, index : index + 1, lanes] = sums[index]
        pg_ref[0, 7:8, lanes] = jnp.zeros((1, 128), jnp.float32)
    for q in range(count):
        rv_ref[0, q * CHUNK : q * CHUNK + CHUNK, :] = columns[q]

    @pl.when(pl.program_id(1) == pl.num_programs(1) - 1)
    def _():
        for q in range(count):
            span = slice(q * CHUNK, q * CHUNK + CHUNK)
            joint = low16(gcb_ref[span, :])
            gc_ref[span, :] += mm(joint, b_ref[span, :])
            gb_ref[span, :] += mm_tn(joint, c_ref[span, :])


def wide_spec(rows, offset=0):
    return pl.BlockSpec((rows, GROUP), lambda i, g: (i, g + offset))


def shared_specs(rows, per, groups):
    row_spec = pl.BlockSpec((rows, NSTATE), lambda i, g: (i, 0))
    return [
        pl.BlockSpec((8, GROUP), lambda i, g: (0, g)),
        row_spec,
        row_spec,
        pl.BlockSpec((NSTATE, rows), lambda i, g: (0, i)),
        pl.BlockSpec((1, rows, per), lambda i, g: (g, i, 0)),
        pl.BlockSpec((1, rows, per), lambda i, g: (g, i, 0)),
        pl.BlockSpec((1, per, rows), lambda i, g: (g, 0, i)),
        pl.BlockSpec((1, per, rows), lambda i, g: (g, 0, i)),
    ]


def ssd_forward(proj, x_at, z_at, par, b_low, c_low, forms, rows):
    width = par.shape[1]
    seqs, groups, per = proj.shape[0] // rows, width // GROUP, GROUP // HEAD_DIM
    total = seqs * rows
    steps = rows // CHUNK
    return pl.pallas_call(
        ssd_forward_kernel,
        grid=(seqs, groups),
        in_specs=[wide_spec(rows, x_at), wide_spec(rows, z_at)] + shared_specs(rows, per, groups),
        out_specs=[
            wide_spec(rows),
            wide_spec(rows),
            pl.BlockSpec((steps - 1, NSTATE, GROUP), lambda i, g: (i, 0, g)),
            pl.BlockSpec((rows, 128), lambda i, g: (i, 0)),
        ],
        out_shape=[
            jax.ShapeDtypeStruct((total, width), jnp.bfloat16),
            jax.ShapeDtypeStruct((total, width), jnp.float32),
            jax.ShapeDtypeStruct((seqs * (steps - 1), NSTATE, width), jnp.bfloat16),
            jax.ShapeDtypeStruct((total, 128), jnp.float32),
        ],
        scratch_shapes=[pltpu.VMEM((rows + 8, GROUP), jnp.float32)],
        compiler_params=pltpu.CompilerParams(dimension_semantics=("arbitrary", "arbitrary")),
        name="ssd_forward",
    )(proj, proj, par, b_low, c_low, b_low.T, *forms)


def ssd_backward(proj, x_at, z_at, par, b_low, c_low, forms, x_low, y, states, mixed_grad, row_coef, rows):
    width = par.shape[1]
    seqs, groups, per = proj.shape[0] // rows, width // GROUP, GROUP // HEAD_DIM
    total = seqs * rows
    steps = rows // CHUNK
    return pl.pallas_call(
        ssd_backward_kernel,
        grid=(seqs, groups),
        in_specs=[wide_spec(rows, x_at), wide_spec(rows, z_at)]
        + shared_specs(rows, per, groups)
        + [
            wide_spec(rows),
            wide_spec(rows),
            pl.BlockSpec((steps - 1, NSTATE, GROUP), lambda i, g: (i, 0, g)),
            wide_spec(rows),
            pl.BlockSpec((rows, 2), lambda i, g: (i, 0)),
        ],
        out_specs=[
            wide_spec(rows),
            wide_spec(rows),
            pl.BlockSpec((1, 8, GROUP), lambda i, g: (i, 0, g)),
            pl.BlockSpec((rows, NSTATE), lambda i, g: (i, 0)),
            pl.BlockSpec((rows, NSTATE), lambda i, g: (i, 0)),
            pl.BlockSpec((1, rows, 128), lambda i, g: (g, i, 0)),
            pl.BlockSpec((1, per, rows), lambda i, g: (g, 0, i)),
            pl.BlockSpec((1, steps, GROUP), lambda i, g: (i, 0, g)),
        ],
        out_shape=[
            jax.ShapeDtypeStruct((total, width), jnp.bfloat16),
            jax.ShapeDtypeStruct((total, width), jnp.bfloat16),
            jax.ShapeDtypeStruct((seqs, 8, width), jnp.float32),
            jax.ShapeDtypeStruct((total, NSTATE), jnp.float32),
            jax.ShapeDtypeStruct((total, NSTATE), jnp.float32),
            jax.ShapeDtypeStruct((groups, total, 128), jnp.float32),
            jax.ShapeDtypeStruct((groups, per, total), jnp.float32),
            jax.ShapeDtypeStruct((seqs, steps, width), jnp.float32),
        ],
        scratch_shapes=[
            pltpu.VMEM((rows + 8, GROUP), jnp.float32),
            pltpu.VMEM((rows + 8, GROUP), jnp.float32),
            pltpu.VMEM((rows, CHUNK), jnp.float32),
        ],
        compiler_params=pltpu.CompilerParams(dimension_semantics=("arbitrary", "arbitrary")),
        name="ssd_backward",
    )(proj, proj, par, b_low, c_low, c_low.T, *forms, x_low, y, states, mixed_grad, row_coef)


def conv_small(values, taps, bias, rows):
    seqs = values.shape[0] // rows
    padded = jnp.pad(values.reshape(seqs, rows, -1), ((0, 0), (KCONV - 1, 0), (0, 0)))
    total = bias
    for tap in range(KCONV):
        total = total + padded[:, tap : tap + rows] * taps[tap]
    return total.reshape(seqs * rows, -1)


def conv_small_back(grad, values, taps, rows):
    seqs = values.shape[0] // rows
    padded = jnp.pad(values.reshape(seqs, rows, -1), ((0, 0), (KCONV - 1, 0), (0, 0)))
    ahead = jnp.pad(grad.reshape(seqs, rows, -1), ((0, 0), (0, KCONV - 1), (0, 0)))
    grads = grad.reshape(seqs, rows, -1)
    back = 0.0
    tap_grads = []
    for tap in range(KCONV):
        shift = KCONV - 1 - tap
        back = back + ahead[:, shift : shift + rows] * taps[tap]
        tap_grads.append(jnp.sum(grads * padded[:, tap : tap + rows], axis=(0, 1)))
    return back.reshape(values.shape), jnp.stack(tap_grads), jnp.sum(grad, axis=0)


def chunk_sums(values, lower):
    size = values.shape[0]
    shape = (CHUNK, CHUNK)
    before = lax.broadcasted_iota(jnp.int32, shape, 0) >= lax.broadcasted_iota(jnp.int32, shape, 1)
    kernel = (before if lower else before.T).astype(jnp.float32)
    return jnp.einsum(
        "ts,qsh->qth", kernel, values.reshape(size // CHUNK, CHUNK, -1), precision=lax.Precision.HIGHEST
    ).reshape(values.shape)


def head_forms(dt_rows, cum):
    per = GROUP // HEAD_DIM
    size, heads = dt_rows.shape

    def by_col(values):
        return values.reshape(size, heads // per, per).transpose(1, 0, 2)

    def by_row(values):
        return values.T.reshape(heads // per, per, size)

    return by_col(dt_rows), by_col(cum), by_row(dt_rows), by_row(cum)


def heads_back(rv, u, e, dt_rows, log_decay, rate, rows):
    per = GROUP // HEAD_DIM
    size, heads = dt_rows.shape
    row_term = rv[:, :, :per].transpose(1, 0, 2).reshape(size, heads)
    leave = rv[:, :, per : 2 * per].transpose(1, 0, 2).reshape(size, heads)
    direct = u.reshape(heads, size).T + leave
    cum_grad = row_term - dt_rows * direct
    ends = jnp.sum((dt_rows * leave).reshape(size // CHUNK, CHUNK, heads), axis=1)
    ends = ends + jnp.sum(e.reshape(size // CHUNK, heads, HEAD_DIM), axis=2)
    log_grad = chunk_sums(cum_grad, False).reshape(size // CHUNK, CHUNK, heads) + ends[:, None, :]
    log_grad = log_grad.reshape(size, heads)
    dt_grad = direct - log_grad * rate
    return dt_grad, jnp.sum(log_grad * log_decay, axis=0)


def rms_scale(values, gain_vec):
    return values * lax.rsqrt(jnp.mean(values * values, axis=-1, keepdims=True) + EPS) * gain_vec


def prepare(proj, x_at, conv_w, conv_b, a_log, dt_bias, rows):
    small = proj[:, x_at + DIN :]
    taps = conv_w[DIN:].T
    pre = conv_small(small[:, : 2 * NSTATE], taps, conv_b[DIN:], rows)
    low = low16(pre * jax.nn.sigmoid(pre))
    dt_pre = small[:, 2 * NSTATE :] + dt_bias
    dt_rows = jax.nn.softplus(dt_pre)
    log_decay = -dt_rows * jnp.exp(a_log)
    forms = head_forms(dt_rows, chunk_sums(log_decay, True))
    return small[:, : 2 * NSTATE], pre, low[:, :NSTATE], low[:, NSTATE:], dt_pre, dt_rows, log_decay, forms


def fetch_weights(in_part, out_part, norm_part, conv_part, bias_part, gain_part):
    return (
        lax.all_gather(in_part, ("wide", "narrow"), axis=0, tiled=True),
        lax.all_gather(out_part, ("wide", "narrow"), axis=0, tiled=True),
        lax.all_gather(norm_part, ("wide", "narrow"), axis=0, tiled=True),
        lax.all_gather(conv_part, ("wide", "narrow"), axis=0, tiled=True),
        lax.all_gather(bias_part, ("wide", "narrow"), axis=0, tiled=True),
        lax.all_gather(gain_part, ("wide", "narrow"), axis=0, tiled=True),
    )


def spread_heads(head_grad, wide_count, narrow_count):
    share_len = head_grad.shape[0] // wide_count
    blocks = jnp.broadcast_to(
        head_grad.reshape(wide_count, 1, share_len), (wide_count, narrow_count, share_len)
    )
    return blocks.reshape(-1)


def settle_grads(
    normed_low,
    proj_grad,
    mixed_low,
    branch_grad,
    norm_term,
    conv_term,
    bias_term,
    gain_term,
    head_terms,
):
    wide_count = lax.axis_size("wide")
    narrow_count = lax.axis_size("narrow")
    heads_laid = [spread_heads(head_term, wide_count, narrow_count) for head_term in head_terms]
    columns = normed_low
    inw_own = lax.psum_scatter(
        lax.dot_general(
            columns, proj_grad, (((0,), (0,)), ((), ())), preferred_element_type=jnp.float32
        ).astype(jnp.bfloat16),
        ("wide", "narrow"),
        scatter_dimension=0,
        tiled=True,
    ).astype(jnp.float32)
    columns = mixed_low
    outw_own = lax.psum_scatter(
        lax.dot_general(
            columns, branch_grad, (((0,), (0,)), ((), ())), preferred_element_type=jnp.float32
        ).astype(jnp.bfloat16),
        ("wide", "narrow"),
        scatter_dimension=0,
        tiled=True,
    ).astype(jnp.float32)
    small_own = (
        lax.psum_scatter(norm_term, ("wide", "narrow"), scatter_dimension=0, tiled=True),
        lax.psum_scatter(conv_term, ("wide", "narrow"), scatter_dimension=0, tiled=True),
        lax.psum_scatter(bias_term, ("wide", "narrow"), scatter_dimension=0, tiled=True),
        lax.psum_scatter(gain_term, ("wide", "narrow"), scatter_dimension=0, tiled=True),
        lax.psum_scatter(heads_laid[0], ("wide", "narrow"), scatter_dimension=0, tiled=True),
        lax.psum_scatter(heads_laid[1], ("wide", "narrow"), scatter_dimension=0, tiled=True),
        lax.psum_scatter(heads_laid[2], ("wide", "narrow"), scatter_dimension=0, tiled=True),
    )
    return (inw_own, outw_own) + tuple(small_own)


def body(
    tokens,
    lengths,
    in_weight,
    out_weight,
    norm_gain,
    conv_weight,
    conv_bias,
    out_gain,
    a_log,
    dt_bias,
    d_skip,
    cotangent,
):
    row_count = tokens.shape[0]
    live_mask = (lax.iota(jnp.int32, row_count) < lengths[0]).astype(jnp.float32)[:, None]
    gathered = fetch_weights(in_weight, out_weight, norm_gain, conv_weight, conv_bias, out_gain)
    head_values = (
        lax.all_gather(a_log, "wide", axis=0, tiled=True),
        lax.all_gather(dt_bias, "wide", axis=0, tiled=True),
        lax.all_gather(d_skip, "wide", axis=0, tiled=True),
    )
    source = tokens.astype(jnp.float32)
    normed, front_back = jax.vjp(rms_scale, source, gathered[2].astype(jnp.float32))
    normed_low = normed.astype(jnp.bfloat16)
    projected = jnp.dot(normed_low, gathered[0], preferred_element_type=jnp.float32)

    conv_w, conv_b = gathered[3].astype(jnp.float32), gathered[4].astype(jnp.float32)
    gain_out = gathered[5].astype(jnp.float32)
    a_full, bias_full, skip_full = head_values
    par = jnp.concatenate(
        [
            conv_w[:DIN].T,
            conv_b[None, :DIN],
            jnp.repeat(skip_full, HEAD_DIM)[None],
            gain_out[None],
            jnp.zeros((1, DIN), jnp.float32),
        ]
    )
    bc_in, bc_pre, b_low, c_low, dt_pre, dt_rows, log_decay, forms = prepare(
        projected, DIN, conv_w, conv_b, a_full, bias_full, row_count
    )
    x_block, z_block = DIN // GROUP, 0
    x_low, y, states, ssq = ssd_forward(
        projected, x_block, z_block, par, b_low, c_low, forms, row_count
    )
    z_part = projected[:, :DIN]
    gated = y * (z_part * jax.nn.sigmoid(z_part))
    inverse = lax.rsqrt(jnp.sum(ssq, axis=1, keepdims=True) / DIN + EPS)
    mixed_low = low16(gated * inverse * gain_out)
    branch = jnp.dot(mixed_low, gathered[1], preferred_element_type=jnp.float32)
    output = (source + live_mask * branch).astype(jnp.bfloat16)
    cot_rows = cotangent.astype(jnp.float32)
    branch_grad = (live_mask * cot_rows).astype(jnp.bfloat16)
    mixed_grad = lax.dot_general(
        branch_grad, gathered[1], (((1,), (1,)), ((), ())), preferred_element_type=jnp.float32
    )
    row_dot = jnp.sum(gated * gain_out * mixed_grad, axis=1, keepdims=True)
    row_coef = jnp.concatenate([inverse, inverse * inverse * inverse * row_dot / DIN], axis=1)
    z_grad, x_grad, par_grad, b_grad, c_grad, rv, u, e = ssd_backward(
        projected, x_block, z_block, par, b_low, c_low, forms, x_low, y, states, mixed_grad, row_coef, row_count
    )
    par_grad = jnp.sum(par_grad, axis=0)
    dt_grad, a_log_grad = heads_back(rv, u, e, dt_rows, log_decay, jnp.exp(a_full), row_count)
    dt_raw_grad = dt_grad * jax.nn.sigmoid(dt_pre)
    bc_sig = jax.nn.sigmoid(bc_pre)
    bc_grad = jnp.concatenate([b_grad, c_grad], axis=1) * (bc_sig * (1.0 + bc_pre * (1.0 - bc_sig)))
    bc_back, bc_taps, bc_bias = conv_small_back(bc_grad, bc_in, conv_w[DIN:].T, row_count)
    conv_w_grad = jnp.concatenate([par_grad[:KCONV], bc_taps], axis=1).T
    conv_b_grad = jnp.concatenate([par_grad[KCONV], bc_bias])
    skip_grad = jnp.sum(par_grad[5].reshape(HEADS, HEAD_DIM), axis=1)
    proj_grad = jnp.concatenate([z_grad, x_grad, low16(bc_back), low16(dt_raw_grad)], axis=1)
    normed_grad = lax.dot_general(
        proj_grad, gathered[0], (((1,), (1,)), ((), ())), preferred_element_type=jnp.float32
    )
    source_grad, normgain_grad = front_back(normed_grad)
    token_grad = (cot_rows + source_grad).astype(jnp.bfloat16)
    owned = settle_grads(
        normed_low,
        proj_grad,
        mixed_low,
        branch_grad,
        normgain_grad,
        conv_w_grad,
        conv_b_grad,
        par_grad[6],
        (a_log_grad, jnp.sum(dt_raw_grad, axis=0), skip_grad),
    )
    return (
        output,
        token_grad,
        owned[0],
        owned[1],
        owned[2],
        owned[3],
        owned[4],
        owned[5],
        owned[6],
        owned[7],
        owned[8],
    )


def solution(mesh):
    in_specs = (
        P(("wide", "narrow"), None),
        P(("wide", "narrow")),
        P(("wide", "narrow"), None),
        P(("wide", "narrow"), None),
        P(("wide", "narrow")),
        P(("wide", "narrow"), None),
        P(("wide", "narrow")),
        P(("wide", "narrow")),
        P("wide"),
        P("wide"),
        P("wide"),
        P(("wide", "narrow"), None),
    )
    out_specs = (
        P(("wide", "narrow"), None),
        P(("wide", "narrow"), None),
        P(("wide", "narrow"), None),
        P(("wide", "narrow"), None),
        P(("wide", "narrow")),
        P(("wide", "narrow"), None),
        P(("wide", "narrow")),
        P(("wide", "narrow")),
        P("wide"),
        P("wide"),
        P("wide"),
    )
    return jax.shard_map(body, mesh=mesh, in_specs=in_specs, out_specs=out_specs, check_vma=False)
```

time: 1740 us -> 1150 us (0.66); the launches traced: 1710 us -> 1150 us
  local copies, waits for them, and re-layouts: 530 us -> 63.6 us
  other arithmetic: 162 us -> 25.8 us
  Pallas kernels: 0 us -> 124 us
  matrix products: 256 us -> 141 us
  waiting for transfers between devices: 552 us -> 591 us
    dynamic_update_slice x12 -> x0, local copies, waits for them, and re-layouts: 412 us -> none  [ssd_mixer(): lax.scan(jax.checkpoint(partial(block_step, rounding=rounding)), zero_sta...]
    pallas_call x0 -> x2, Pallas kernels: none -> 124 us  [the longest x1 91.3 us: ssd_backward(): pl.pallas_call(ssd_backward_kernel, grid=(seqs, groups), in_specs=[wide_s...]
    dot_general x24 -> x2, matrix products: 105 us -> 0.74 us  [chunk_sums(): jnp.einsum('ts,qsh->qth', kernel, values.reshape(size // CHUNK, CHUNK, -1...]
    reduce_sum x8 -> x7, other arithmetic: 51.6 us -> 6.71 us  [the longest x1 1.94 us: conv_small_back(): jnp.sum(grad, axis=0)]
    mul x4 -> x2, other arithmetic: 37.3 us -> 1.18 us  [the longest x1 1.12 us: prepare(): log_decay = -dt_rows * jnp.exp(a_log)]
    all_gather x1, waiting for transfers between devices: 0.02 us -> 24.2 us  [fetch_weights(): lax.all_gather(out_part, ('wide', 'narrow'), axis=0, tiled=True)]
    add_any x7 -> x0, other arithmetic: 21.3 us -> none  [the longest x2 15.1 us: ssd_mixer(): conv_out = conv_out + padded[tap_idx:tap_idx + seq_len] * conv_w[:, tap_idx]]
    squeeze x8 -> x0, local copies, waits for them, and re-layouts: 19 us -> none  [ssd_mixer(): lax.scan(jax.checkpoint(partial(block_step, rounding=rounding)), zero_sta...]
  transfers between devices with their start and end apart: 5 -> 5, of which waited for: 3 -> 4; matrix products, arithmetic and copies ran while one was open for 29% -> 17% of each run, Pallas kernels for 0% -> 3%
where the time goes in v2:
time: 1150 us
  waiting for transfers between devices  591 us (51%)
  blocking collectives  185 us (16%)
  matrix products  141 us (12%)
  Pallas kernels  124 us (11%)
  local copies, waits for them, and re-layouts  63.6 us (6%)
  other arithmetic  25.8 us (2%)
  between operations  15.8 us (1%)
    reduce_scatter x1, waiting for transfers between devices, settle_grads(): lax.psum_scatter(lax.dot_general(columns, proj_grad, (((0,), (0,)), ((),...  375 us
    reduce_scatter x1, waiting for transfers between devices, settle_grads(): lax.psum_scatter(lax.dot_general(columns, branch_grad, (((0,), (0,)), (()...  135 us
    unnamed x3, blocking collectives  99.9 us
    pallas_call x1, Pallas kernels, ssd_backward(): pl.pallas_call(ssd_backward_kernel, grid=(seqs, groups), in_specs=[wide_s...  91.3 us
    all_gather x1, waiting for transfers between devices, fetch_weights(): lax.all_gather(in_part, ('wide', 'narrow'), axis=0, tiled=True)  54.9 us
    all_gather x1, blocking collectives, fetch_weights(): lax.all_gather(conv_part, ('wide', 'narrow'), axis=0, tiled=True)  43.3 us
    all_gather x1, blocking collectives, fetch_weights(): lax.all_gather(gain_part, ('wide', 'narrow'), axis=0, tiled=True)  42.1 us
    pallas_call x1, Pallas kernels, ssd_forward(): pl.pallas_call(ssd_forward_kernel, grid=(seqs, groups), in_specs=[wide_sp...  32.6 us
  transfers between devices with their start and end apart: 5, of which 4 were waited for; matrix products, arithmetic and copies ran while one was open for 17% of the time, Pallas kernels for 3%

profile of v2, /device:TPU:1, one launch (start us, length us, event | category | flops | bytes accessed | tf_op | source)
XLA Modules:
  0.0 1145.8 jit_solution(10815997707364118039)
XLA Ops:
  8.7 0.9 dynamic-update-slice
  9.6 0.8 dynamic-update-slice.1
  10.4 43.7 %all-reduce.16 = (bf16[2048]{0:T(1024)(128)(2,1)S(1)}, bf16[4352]{0:T(1024)(128)(2,1)S(1)}) all-reduce(bf16[2048]{0:T(1024)(128)(2,1)S(1)} %dynamic-update-slice, bf16[4352]{0:T(1024)(128)(2,1)S(1)} %dynamic-update-slice.1), channel_id=1, replica_groups=mesh['wide'=8,'narrow'=4] {'wide','narrow'}, use_global_device_ids=true, to_apply=%add.2 | all-reduce | flops 6400 | bytes 25600
  54.8 43.3 %all-gather = bf16[32,136,4]{1,2,0:T(4,128)(2,1)S(1)} all-gather(bf16[1,136,4]{1,2,0:T(4,128)(2,1)} %bitcast.154), channel_id=1, replica_groups=mesh['wide'=8,'narrow'=4] {'wide','narrow'}, dimensions={0}, use_global_device_ids=true | all-gather | bytes 35904 | tf_op jit(solution)/shard_map/all_gather | solution.py:412
  98.3 1.2 dynamic-slice
  100.2 0.9 dynamic-update-slice.2
  102.7 14.0 %all-reduce.15 = (f32[64]{0:T(128)S(1)}, f32[64]{0:T(128)S(1)}, f32[64]{0:T(128)S(1)}) all-reduce(f32[64]{0:T(128)S(1)} %dynamic-update-slice.2, f32[64]{0:T(128)S(1)} %dynamic-update-slice.3, f32[64]{0:T(128)S(1)} %dynamic-update-slice.4), channel_id=1, replica_groups=mesh['wide'=8,'narrow'=4] {'wide'}, use_global_device_ids=true, to_apply=%add.4 | all-reduce | flops 192 | bytes 1536
  116.9 42.1 %all-gather.1 = bf16[32,1,128]{2,1,0:T(2,128)(2,1)S(1)} all-gather(bf16[1,1,128]{2,1,0:T(2,128)(2,1)} %bitcast.156), channel_id=1, replica_groups=mesh['wide'=8,'narrow'=4] {'wide','narrow'}, dimensions={0}, use_global_device_ids=true | all-gather | bytes 8448 | tf_op jit(solution)/shard_map/all_gather | solution.py:414
  159.8 2.1 fusion.6
  162.0 54.9 %all-gather.5.cloned.1.call-done = bf16[2048,8512]{1,0:T(8,128)(2,1)} async-done(((bf16[64,8512]{1,0:T(8,128)(2,1)}), bf16[2048,8512]{1,0:T(8,128)(2,1)}) %all-gather.5.cloned.1.call-update) | async-done | bytes 34865168 | tf_op jit(solution)/shard_map/all_gather | solution.py:409
  216.8 26.0 %fusion.15 = f32[512,8512]{0,1:T(8,128)} fusion(bf16[2048,8512]{1,0:T(8,128)(2,1)} %all-gather.5.cloned.1.call-done, bf16[512,2048]{1,0:T(8,128)(2,1)} %param.12, f32[2048]{0:T(1024)S(1)} %convert_element_type.73, f32[512]{0:T(512)S(1)} %fusion.41), kind=kOutput, calls=%fused_computation.36 | convolution fusion | flops 17855152128 | bytes 54405120 | tf_op jit(solution)/shard_map/dot_general | solution.py:495
  242.9 17.9 %copy.121.xin_ref.z_ref = f32[512,8512]{1,0:T(8,128)} copy(f32[512,8512]{0,1:T(8,128)} %fusion.15) | data formatting | bytes 34865152 | tf_op jit(solution)/shard_map/dot_general | solution.py:495
  260.8 1.1 slice_bitcast_fusion.2
  261.9 1.7 fusion.27
  265.9 1.1 negate_multiply_fusion
  267.2 2.6 copy.115
  270.3 2.6 copy.118
  274.5 32.6 %ssd_forward.1 = (bf16[512,4096]{1,0:T(8,128)(2,1)}, f32[512,4096]{1,0:T(8,128)}, bf16[3,128,4096]{2,1,0:T(8,128)(2,1)}, f32[512,128]{1,0:T(8,128)}) custom-call(f32[512,8512]{1,0:T(8,128)} %copy.121.xin_ref.z_ref, f32[512,8512]{1,0:T(8,128)} %copy.121.xin_ref.z_ref, f32[8,4096]{1,0:T(8,128)} %concatenate.26.par_ref, bf16[512,128]{1,0:T(8,128)(2,1)} %copy.123.b_ref, ...), custom_call_target="tpu_custom_call" | custom-call | tf_op jit(solution)/shard_map/ssd_forward/pallas_call | solution.py:261
  307.1 1.1 reduce_sum.150
  308.2 24.2 %all-gather.7.cloned.1.call-done = bf16[4096,2048]{1,0:T(8,128)(2,1)} async-done(((bf16[128,2048]{1,0:T(8,128)(2,1)}), bf16[4096,2048]{1,0:T(8,128)(2,1)}) %all-gather.7.cloned.1.call-update) | async-done | bytes 16777232 | tf_op jit(solution)/shard_map/all_gather | solution.py:410
  332.4 20.5 %multiply_reduce_fusion = (f32[512]{0:T(512)S(1)}, f32[512,4096]{1,0:T(8,128)}) fusion(f32[4096]{0:T(1024)S(1)} %bitcast.139, f32[512,4096]{1,0:T(8,128)} %get-tuple-element.23.y_ref, f32[512,8512]{1,0:T(8,128)} %copy.121.xin_ref.z_ref, bf16[4096,2048]{1,0:T(8,128)(2,1)} %all-gather.7.cloned.1.call-done, bf16[512,2048]{1,0:T(8,128)(2,1)} %param.23, ...), kind=kOutput, calls=%fused_computation.3 | convolution fusion | flops 8609857536 | bytes 44060672 | tf_op jit(solution)/shard_map/dot_general | solution.py:524
  352.9 0.9 copy.130.rc_ref
  353.8 91.3 %ssd_backward.1 = (bf16[512,4096]{1,0:T(8,128)(2,1)}, bf16[512,4096]{1,0:T(8,128)(2,1)}, f32[1,8,4096]{2,1,0:T(8,128)}, f32[512,128]{1,0:T(8,128)}, f32[512,128]...) custom-call(f32[512,8512]{1,0:T(8,128)} %copy.121.xin_ref.z_ref, ...), custom_call_target="tpu_custom_call" | custom-call | tf_op jit(solution)/shard_map/ssd_backward/pallas_call | solution.py:288
  445.1 1.1 copy.132
  446.2 1.1 copy.131
  447.3 0.9 slice_bitcast_fusion.4
  448.2 1.9 fusion.44
  450.1 1.2 multiply_reduce_fusion.4
  452.1 18.4 %convolution_convert_fusion.1 = bf16[4096,2048]{1,0:T(8,128)(2,1)} fusion(bf16[512,2048]{1,0:T(8,128)(2,1)} %param.23, f32[512]{0:T(512)S(1)} %fusion.40, f32[4096]{0:T(1024)S(1)} %bitcast.140, f32[512]{0:T(512)S(1)} %add_rsqrt_fusion, f32[512,4096]{1,0:T(8,128)} %get-tuple-element.23.y_ref, f32[512,8512]{1,0:T(8,128)} %copy.121.xin_ref.z_ref), kind=kOutput, calls=%fused_computation.1 | convolution fusion | flops 8618246144 | bytes 35672064 | tf_op jit(solution)/shard_map/dot_general | solution.py:451
  470.6 8.1 slice_bitcast_fusion.1
  478.7 3.1 copy.134
  482.1 2.9 copy.136
  485.1 1.0 reshape.206
  486.2 1.0 reshape.211
  489.2 2.4 fusion.33
  491.6 0.8 copy.141
  492.4 1.6 fusion.45
  494.0 26.9 %convolution_convert_fusion = bf16[2048,8512]{1,0:T(8,128)(2,1)} fusion(bf16[512,64]{1,0:T(8,128)(2,1)S(1)} %get-tuple-element.55, bf16[512,256]{1,0:T(8,128)(2,1)} %copy.141, bf16[512,4096]{1,0:T(8,128)(2,1)} %get-tuple-element.28, bf16[512,4096]{1,0:T(8,128)(2,1)} %get-tuple-element.27, bf16[512,2048]{1,0:T(8,128)(2,1)S(1)} %copy-done, ...), kind=kOutput, calls=%fused_computation | convolution fusion | flops 17907449856 | bytes 45688832 | tf_op jit(solution)/shard_map/dot_general | solution.py:442
  521.9 1.1 slice_reduce_fusion
  523.5 28.3 %fusion.3 = (f32[2048]{0:T(1024)S(1)}, f32[512]{0:T(512)S(1)}, f32[512,2048]{1,0:T(8,128)}) fusion(bf16[512,2048]{1,0:T(8,128)(2,1)S(1)} %copy-done, f32[512]{0:T(512)S(1)} %copy-done.10, f32[2048]{0:T(1024)S(1)} %convert_element_type.73, bf16[2048,8512]{1,0:T(8,128)(2,1)} %all-gather.5.cloned.1.call-done, bf16[512,64]{1,0:T(8,128)(2,1)S(1)} %get-tuple-element.55, ...), kind=kOutput, calls=%fused_computation.17 | convolution fusion | flops 17893160960 | bytes 49893376 | tf_op jit(solution)/shard_map/dot_general | solution.py:542
  551.8 42.3 %all-reduce.14 = (f32[2048]{0:T(1024)S(1)}, f32[4352]{0:T(1024)S(1)}, f32[4096]{0:T(1024)S(1)}, f32[256]{0:T(256)S(1)}, f32[256]{0:T(256)S(1)}, /*index=5*/f32[256]{0:T(256)S(1)}) all-reduce(f32[2048]{0:T(1024)S(1)} %get-tuple-element.35, ...), channel_id=4, replica_groups=mesh['wide'=8,'narrow'=4] {'wide','narrow'}, use_global_device_ids=true, to_apply=%region_9.10.clone | all-reduce | flops 11264 | bytes 90112
  597.6 5.4 fusion.5
  603.1 19.7 %fusion.7 = bf16[512,2048]{1,0:T(8,128)(2,1)} fusion(bf16[512,2048]{1,0:T(8,128)(2,1)S(1)} %copy-done, bf16[4096,2048]{1,0:T(8,128)(2,1)} %all-gather.7.cloned.1.call-done, f32[512]{0:T(512)S(1)} %copy-done.16, f32[4096]{0:T(1024)S(1)} %bitcast.141, f32[512]{0:T(512)S(1)} %add_rsqrt_fusion, f32[512,4096]{1,0:T(8,128)} %get-tuple-element.23.y_ref, ...), kind=kOutput, calls=%fused_computation.21 | convolution fusion | flops 8610906112 | bytes 37769216 | tf_op jit(solution)/shard_map/dot_general | solution.py:520
  622.7 1.4 constant_dynamic-slice_fusion
  624.1 135.2 %reduce-scatter.6.cloned.1.call-done = bf16[128,2048]{1,0:T(8,128)(2,1)} async-done(((bf16[4096,2048]{1,0:T(8,128)(2,1)}), bf16[128,2048]{1,0:T(8,128)(2,1)}) %reduce-scatter.6.cloned.1.call-update) | async-done | bytes 524304 | tf_op jit(solution)/shard_map/reduce_scatter | solution.py:450
  759.3 2.1 convert_element_type.90
  761.4 374.8 %reduce-scatter.4.cloned.1.call-done = bf16[64,8512]{1,0:T(8,128)(2,1)} async-done(((bf16[2048,8512]{1,0:T(8,128)(2,1)}), bf16[64,8512]{1,0:T(8,128)(2,1)}) %reduce-scatter.4.cloned.1.call-update) | async-done | bytes 1089552 | tf_op jit(solution)/shard_map/reduce_scatter | solution.py:441
  1136.3 2.7 convert_element_type.88
  (114 shorter events, 17.0 us)
Async XLA Ops:
  7.2 209.7 %all-gather.5.cloned.1.call-start = ((), (), s32[]{:S(2)}) async-start(), calls=%async_computation.2 | async-start | bytes 36225024 | tf_op jit(solution)/shard_map/all_gather | solution.py:409
  7.9 324.5 %all-gather.7.cloned.1.call-start = ((), (), s32[]{:S(2)}) async-start(), calls=%async_computation.3 | async-start | bytes 17301504 | tf_op jit(solution)/shard_map/all_gather | solution.py:410
  8.7 614.1 %all-reduce.19.cloned.1.call-start = ((), (), s32[]{:S(2)}) async-start(), calls=%async_computation.6 | async-start | bytes 139264
  116.7 149.2 %copy-start.12 = (f32[64]{0:T(128)}, f32[64]{0:T(128)S(1)}, u32[]{:S(2)}) copy-start(f32[64]{0:T(128)S(1)} %get-tuple-element.49) | copy-start | bytes 772
  116.9 149.0 %copy-start.13 = (f32[64]{0:T(128)}, f32[64]{0:T(128)S(1)}, u32[]{:S(2)}) copy-start(f32[64]{0:T(128)S(1)} %exp.24) | copy-start | bytes 772
  159.0 293.1 %copy-start.4 = (f32[32,1,128]{2,1,0:T(1,128)}, f32[32,1,128]{2,1,0:T(1,128)S(1)}, u32[]{:S(2)}) copy-start(f32[32,1,128]{2,1,0:T(1,128)S(1)} %get-tuple-element.73) | copy-start | bytes 49156
  159.8 292.3 %copy-start.15 = (f32[512]{0:T(512)}, f32[512]{0:T(512)S(1)}, u32[]{:S(2)}) copy-start(f32[512]{0:T(512)S(1)} %fusion.40) | copy-start | bytes 6148
  161.9 81.0 %copy-start.2 = (f32[512]{0:T(512)}, f32[512]{0:T(512)S(1)}, u32[]{:S(2)}) copy-start(f32[512]{0:T(512)S(1)} %fusion.6) | copy-start | bytes 6148
  161.9 81.0 %copy-start.9 = (f32[512]{0:T(512)}, f32[512]{0:T(512)S(1)}, u32[]{:S(2)}) copy-start(f32[512]{0:T(512)S(1)} %fusion.41) | copy-start | bytes 6148
  161.9 99.9 %copy-start.6 = (f32[1,256]{1,0:T(1,128)}, f32[1,256]{1,0:T(1,128)S(1)}, u32[]{:S(2)}) copy-start(f32[1,256]{1,0:T(1,128)S(1)} %get-tuple-element.75) | copy-start | bytes 3076
  161.9 99.9 %copy-start.7 = (f32[1,256]{1,0:T(1,128)}, f32[1,256]{1,0:T(1,128)S(1)}, u32[]{:S(2)}) copy-start(f32[1,256]{1,0:T(1,128)S(1)} %get-tuple-element.76) | copy-start | bytes 3076
  162.0 99.9 %copy-start.8 = (f32[1,256]{1,0:T(1,128)}, f32[1,256]{1,0:T(1,128)S(1)}, u32[]{:S(2)}) copy-start(f32[1,256]{1,0:T(1,128)S(1)} %get-tuple-element.77) | copy-start | bytes 3076
  452.0 307.3 %reduce-scatter.6.cloned.1.call-start = ((), (), s32[]{:S(2)}) async-start(), calls=%async_computation.5 | async-start | bytes 17301504 | tf_op jit(solution)/shard_map/reduce_scatter | solution.py:450
  470.6 665.7 %reduce-scatter.4.cloned.1.call-start = ((), (), s32[]{:S(2)}) async-start(), calls=%async_computation.4 | async-start | bytes 36225024 | tf_op jit(solution)/shard_map/reduce_scatter | solution.py:441
  478.7 15.3 %copy-start = (bf16[512,2048]{1,0:T(8,128)(2,1)S(1)}, bf16[512,2048]{1,0:T(8,128)(2,1)}, u32[]{:S(2)}) copy-start(bf16[512,2048]{1,0:T(8,128)(2,1)} %param.12) | copy-start | bytes 6291460
  520.9 0.7 copy-start.14
  520.9 2.5 copy-start.11
  520.9 2.6 copy-start.1
  520.9 2.6 copy-start.10
  523.5 74.1 %copy-start.3 = (f32[512]{0:T(512)S(1)}, f32[512]{0:T(512)}, u32[]{:S(2)}) copy-start(f32[512]{0:T(512)} %copy-done.2) | copy-start | bytes 6148
  551.8 51.3 %copy-start.5 = (f32[32,1,128]{2,1,0:T(1,128)S(1)}, f32[32,1,128]{2,1,0:T(1,128)}, u32[]{:S(2)}) copy-start(f32[32,1,128]{2,1,0:T(1,128)} %copy-done.4) | copy-start | bytes 49156
  551.8 51.3 %copy-start.16 = (f32[512]{0:T(512)S(1)}, f32[512]{0:T(512)}, u32[]{:S(2)}) copy-start(f32[512]{0:T(512)} %copy-done.15) | copy-start | bytes 6148
Sparse Core Ops, SparseCore 0:
  10.8 205.9 all-gather.4
  219.7 112.6 all-gather.6
  452.2 119.3 all-reduce.18
  573.8 185.5 reduce-scatter.5
  761.5 374.7 reduce-scatter.3
